TPU v7x, 32 devices: a whole 2x2x4 slice. The times are simulated.
32 devices in a mesh: seq: 8 (over z, x), chan: 4 (over y, core).
Axes of the slice: x: 2, y: 2, z: 4, core: 2. Of those that a mesh axis runs over, the one named last changes fastest.
Arguments:
- query_gate: bfloat16 [4096, 8192], P('seq', 'chan'), may hold values from -23 to 23
- key_gate: bfloat16 [4096, 8192], P('seq', 'chan'), may hold values from -6 to 6
- value_input: bfloat16 [4096, 8192], P('seq', 'chan'), may hold values from -6 to 6
- filter_taps: bfloat16 [4096, 128], P('seq', 'chan'), may hold values from -1 to 1
- norm_gain: float32 [8192], P('chan'), may hold values from 0.5 to 1.5
Outputs:
- gated: bfloat16 [4096, 8192], P('seq', 'chan')
- normed: bfloat16 [4096, 8192], P('seq', 'chan')
All inputs are finite; a program needn't handle non-finite values.
Results may differ from a plain program's by a relative error of at most 0.01.
Values may be sent and summed in bfloat16 or wider, within the bound.
No kernel may reach another device: no remote copies, remote signals or barrier semaphores. Data moves between devices by JAX's collectives and lax.ppermute only.
A program may use at most 64 MiB of HBM per device.

v0:
```python
import functools
import math

import jax
import jax.numpy as jnp
from jax import lax
from jax.experimental import pallas as pl
from jax.experimental.pallas import tpu as pltpu
from jax.sharding import PartitionSpec as P


D = 8192
GROUPS = 128


norm_eps = 1e-05


def angle_table(rows_count, cols_count, period):
    row_ids = lax.iota(jnp.int32, rows_count)
    col_ids = lax.iota(jnp.int32, cols_count)
    phases = row_ids[:, None] * col_ids[None, :] % period
    return phases.astype(jnp.float32) * (2.0 * math.pi / period)


def block_matrix(rows_count, cols_count, period):
    phases = angle_table(rows_count, cols_count, period)
    return jnp.stack([jnp.cos(phases), -jnp.sin(phases)]).astype(jnp.bfloat16)


def line_matrix(length, direction):
    phases = angle_table(length, length, length)
    cosine = jnp.cos(phases)
    sine_part = jnp.sin(phases) * direction
    upper = jnp.concatenate([cosine, sine_part], axis=1)
    lower = jnp.concatenate([-sine_part, cosine], axis=1)
    return jnp.concatenate([upper, lower], axis=0).astype(jnp.bfloat16)


def twiddle_minor(real_in, imag_in, period, direction):
    phases = angle_table(real_in.shape[1], real_in.shape[2], period)
    cosine = jnp.cos(phases)[None, :, :]
    sine_part = direction * jnp.sin(phases)[None, :, :]
    real_part = real_in * cosine - imag_in * sine_part
    imaginary = imag_in * cosine + real_in * sine_part
    return (real_part, imaginary)


def spectrum_minor(rows_in, first_matrix, right_forward, periods):
    spread = jnp.einsum("cab,rak->rckb", rows_in, first_matrix, preferred_element_type=jnp.float32)
    real_part, imaginary = twiddle_minor(spread[0], spread[1], periods, -1.0)
    joined = jnp.concatenate(
        [real_part.astype(jnp.bfloat16), imaginary.astype(jnp.bfloat16)], axis=2
    )
    return jnp.einsum("ckb,bm->ckm", joined, right_forward, preferred_element_type=jnp.float32)


def dense_body(query_gate, key_gate, value_input, filter_taps, norm_gain):
    tokens, channels = key_gate.shape
    blocks = lax.axis_size("seq")
    periods = 2 * tokens * blocks
    product = (key_gate.astype(jnp.float32) * value_input.astype(jnp.float32)).astype(jnp.bfloat16)
    first_matrix = block_matrix(blocks, 2 * blocks, 2 * blocks)
    last_matrix = block_matrix(2 * blocks, blocks, 2 * blocks)
    line_forward = line_matrix(tokens, 1.0)
    line_backward = line_matrix(tokens, -1.0)
    width_here = channels // blocks
    group_width = D // GROUPS
    repeat_count = max(1, group_width // width_here)
    taps_wide = jnp.repeat(filter_taps, repeat_count, axis=1)
    data_major = jnp.transpose(product)
    taps_major = jnp.transpose(taps_wide)
    data_whole, taps_whole = (
        lax.all_to_all(data_major, "seq", split_axis=0, concat_axis=1, tiled=True),
        lax.all_to_all(taps_major, "seq", split_axis=0, concat_axis=1, tiled=True),
    )
    taps_cols = taps_whole.shape[0]
    data_rows = data_whole.reshape(width_here, blocks, tokens)
    taps_rows = taps_whole.reshape(taps_cols, blocks, tokens)
    right_forward = jnp.transpose(line_forward)
    right_backward = jnp.transpose(line_backward)
    spectrum = spectrum_minor(data_rows, first_matrix, right_forward, periods)
    taps_spectrum = spectrum_minor(taps_rows, first_matrix, right_forward, periods)
    grouped = spectrum.reshape(taps_cols, width_here // taps_cols, 2 * blocks, 2 * tokens)
    spec_real = grouped[..., :tokens]
    spec_imag = grouped[..., tokens:]
    filter_real = taps_spectrum[:, None, :, :tokens]
    filter_imag = taps_spectrum[:, None, :, tokens:]
    filtered_real = (spec_real * filter_real - spec_imag * filter_imag).astype(jnp.bfloat16)
    filtered_imag = (spec_real * filter_imag + spec_imag * filter_real).astype(jnp.bfloat16)
    filtered = jnp.concatenate([filtered_real, filtered_imag], axis=3).reshape(
        width_here, 2 * blocks, 2 * tokens
    )
    inverted = jnp.einsum(
        "ckm,mb->ckb", filtered, right_backward, preferred_element_type=jnp.float32
    )
    back_real, back_imag = twiddle_minor(
        inverted[..., :tokens], inverted[..., tokens:], periods, 1.0
    )
    returned = jnp.stack([back_real, back_imag]).astype(jnp.bfloat16)
    summed = jnp.einsum("rckb,rka->cab", returned, last_matrix, preferred_element_type=jnp.float32)
    local_blocks = (
        (summed * (1.0 / periods)).astype(jnp.bfloat16).reshape(width_here, blocks * tokens)
    )
    convolved_major = lax.all_to_all(local_blocks, "seq", split_axis=1, concat_axis=0, tiled=True)
    convolved = jnp.transpose(convolved_major)
    gated_full = query_gate.astype(jnp.float32) * convolved.astype(jnp.float32)
    partial_squares = jnp.sum(gated_full * gated_full, axis=1)
    square_sum = lax.psum(partial_squares, "chan")
    inverse_rms = lax.rsqrt(square_sum / D + norm_eps)
    normed = gated_full * inverse_rms[:, None] * norm_gain[None, :]
    return (gated_full.astype(jnp.bfloat16), normed.astype(jnp.bfloat16))


LANES = 128
HALF = 256
VMEM_BYTES = 20 << 20
SMALL_BYTES = 10 << 20
FIRST_BYTES = 62 << 20
PRODUCT_BYTES = 58 << 20
ANYWHERE = pl.BlockSpec(memory_space=pl.ANY)
ORDERS = (
    (6, 7, 4, 5, 2, 3, 1),
    (1, 2, 3, 4, 5, 6, 7),
    (1, 2, 3, 4, 5, 6, 7),
    (1, 2, 3, 4, 5, 6, 7),
)
FINISH_ROWS = 256


def pairs_of(blocks, delta):
    return [(source, source ^ delta) for source in range(blocks)]


def tap_rows_of(taps_ref, rows_ref, blocks):
    groups, count = taps_ref.shape[0] // blocks, taps_ref.shape[1] // LANES
    mirror = lax.broadcasted_iota(jnp.int32, (LANES, LANES), 0) + lax.broadcasted_iota(
        jnp.int32, (LANES, LANES), 1
    )
    mirror = (mirror == LANES - 1).astype(jnp.float32).astype(jnp.bfloat16)
    for part in range(count):
        line = taps_ref[:, pl.ds(part * LANES, LANES)]
        line = jnp.dot(line, mirror, preferred_element_type=jnp.float32)
        for block in range(blocks):
            rows_ref[block, pl.ds(part * groups, groups), :] = line[block * groups : (block + 1) * groups]


def product_kernel(blocks, deltas, tokens, with_taps, seq_ref, *refs):
    count = len(deltas)
    keys, values = refs[:count], refs[count : 2 * count]
    outs = refs[-count - 1 : -1] if with_taps else refs[-count:]
    if with_taps:
        taps_ref, rows_ref = refs[2 * count], refs[-1]
        tap_rows_of(taps_ref, rows_ref, blocks)
    for index, delta in enumerate(deltas):
        wide = keys[index][...].astype(jnp.float32) * values[index][...].astype(jnp.float32)
        outs[index][pl.ds(0, tokens), :] = wide.astype(jnp.bfloat16)
        if with_taps:
            lines = rows_ref[seq_ref[0] ^ delta]
            outs[index][pl.ds(tokens, lines.shape[0]), :] = lines.astype(jnp.bfloat16)


def make_product(seq_index, key_gate, value_input, taps, blocks, deltas, chunk, chunks, vmem_bytes):
    tokens, count = key_gate.shape[0], len(deltas)
    with_taps = taps is not None
    tap_rows = taps.size // (blocks * LANES) if with_taps else 0
    rows = tokens + tap_rows
    column = [
        pl.BlockSpec((tokens, LANES), functools.partial(column_map, delta, chunk, chunks))
        for delta in deltas
    ]
    taps_spec = [pl.BlockSpec(taps.shape, lambda step, seq_ref: (0, 0))] if with_taps else []
    scratch = [pltpu.VMEM((blocks, tap_rows, LANES), jnp.float32)] if with_taps else []
    made = pl.pallas_call(
        functools.partial(product_kernel, blocks, deltas, tokens, with_taps),
        out_shape=[jax.ShapeDtypeStruct((rows, LANES), jnp.bfloat16)] * count,
        grid_spec=pltpu.PrefetchScalarGridSpec(
            num_scalar_prefetch=1,
            grid=(1,),
            in_specs=column + column + taps_spec,
            out_specs=[pl.BlockSpec((rows, LANES), lambda step, seq_ref: (0, 0))] * count,
            scratch_shapes=scratch,
        ),
        cost_estimate=pl.CostEstimate(
            flops=tokens * LANES * count, bytes_accessed=6 * tokens * LANES * count, transcendentals=0
        ),
        compiler_params=pltpu.CompilerParams(vmem_limit_bytes=vmem_bytes),
    )(seq_index, *[key_gate] * count, *[value_input] * count, *([taps] if with_taps else []))
    return dict(zip(deltas, made))


def column_map(delta, chunk, chunks, step, seq_ref):
    return (0, (seq_ref[0] ^ delta) * chunks + chunk)


def fill_table(table, lines, block, per_chunk):
    def one_line(group, index):
        at = index % 4
        return lines[group, block + 1 + (index - at) // 4, pl.ds(at, 1), :]

    for group in range(per_chunk):
        for index in range(-1, 4):
            base = jnp.concatenate([one_line(group, index), one_line(group, index - 1)], axis=1)
            wide = jnp.broadcast_to(base, (LANES, 2 * LANES))
            turned = pltpu.roll(wide, 1, 1, stride=1, stride_axis=0)
            square = turned[:, LANES:].astype(jnp.bfloat16)
            for row, col, want in (
                (0, 0, 0), (1, 0, 1), (0, 1, -1), (1, 1, 0),
                (0, 2, 2), (1, 2, 3), (0, 3, 1), (1, 3, 2),
            ):
                if want == index:
                    rows = pl.ds(group * HALF + row * LANES, LANES)
                    table[rows, pl.ds(block * 2 * HALF + col * LANES, LANES)] = square


def conv_kernel(blocks, per_chunk, chunk, seq_ref, *refs):
    pieces, taps, outs = refs[:blocks], refs[blocks : 2 * blocks], refs[-blocks - 4 : -4]
    past, table, lines, results = refs[-4:]
    last = 2 * blocks - 1
    lines[...] = jnp.zeros_like(lines)
    past[pl.ds(2 * blocks * HALF, HALF), :] = jnp.zeros((HALF, LANES), jnp.bfloat16)
    for delta in range(blocks):
        source = seq_ref[0] ^ delta
        rows = taps[delta][...].astype(jnp.float32)
        groups = rows.shape[0] // 4
        for group in range(per_chunk):
            for part in range(4):
                row = part * groups + chunk * per_chunk + group
                lines[group, source + 1, pl.ds(part, 1), :] = rows[row : row + 1]
        for part in range(2):
            place = pl.multiple_of((last - part - 2 * source) * HALF, HALF)
            past[pl.ds(place, HALF), :] = pieces[delta][pl.ds(part * HALF, HALF), :]
    lane = lax.broadcasted_iota(jnp.int32, (HALF, LANES), 1) * per_chunk // LANES
    for target in range(blocks):
        fill_table(table, lines, target, per_chunk)
        depth = (target + 1) * 2 * HALF
        left = past[pl.ds((last - 2 * target) * HALF, depth), :]
        right = past[pl.ds((last - 2 * target - 1) * HALF, depth), :]
        total = jnp.dot(
            table[:, pl.ds(0, depth)],
            jnp.concatenate([left, right], axis=1),
            preferred_element_type=jnp.float32,
        )
        for part in range(2):
            columns = slice(part * LANES, (part + 1) * LANES)
            chosen = total[:HALF, columns]
            for group in range(1, per_chunk):
                chosen = jnp.where(lane == group, total[group * HALF : (group + 1) * HALF, columns], chosen)
            results[target, pl.ds(part * HALF, HALF), :] = chosen.astype(jnp.bfloat16)
    for delta in range(blocks):
        outs[delta][...] = results[seq_ref[0] ^ delta]


def make_conv(seq_index, pieces, taps, blocks, tokens, groups, chunk, chunks, after):
    per_chunk = groups // chunks
    tap_rows = taps[0].shape[0] - tokens
    flops = 4 * HALF * HALF * HALF * per_chunk * blocks * (blocks + 1)
    return pl.pallas_call(
        functools.partial(conv_kernel, blocks, per_chunk, chunk),
        out_shape=[jax.ShapeDtypeStruct((tokens, LANES), jnp.bfloat16)] * blocks,
        grid_spec=pltpu.PrefetchScalarGridSpec(
            num_scalar_prefetch=1,
            grid=(1,),
            in_specs=[pl.BlockSpec((tokens, LANES), lambda step, seq_ref: (0, 0))] * blocks
            + [pl.BlockSpec((tap_rows, LANES), lambda step, seq_ref: (tokens // tap_rows, 0))] * blocks
            + [ANYWHERE] * len(after),
            out_specs=[pl.BlockSpec((tokens, LANES), lambda step, seq_ref: (0, 0))] * blocks,
            scratch_shapes=[
                pltpu.VMEM(((2 * blocks + 1) * HALF, LANES), jnp.bfloat16),
                pltpu.VMEM((per_chunk * HALF, 2 * blocks * HALF), jnp.bfloat16),
                pltpu.VMEM((per_chunk, blocks + 1, 8, LANES), jnp.float32),
                pltpu.VMEM((blocks, tokens, LANES), jnp.bfloat16),
            ],
        ),
        cost_estimate=pl.CostEstimate(
            flops=flops, bytes_accessed=4 * blocks * tokens * LANES, transcendentals=0
        ),
        compiler_params=pltpu.CompilerParams(vmem_limit_bytes=VMEM_BYTES),
    )(seq_index, *pieces, *taps, *after)


def squares_kernel(blocks, seq_ref, *refs):
    gates, pieces, carried, out = refs[:blocks], refs[blocks : 2 * blocks], refs[2 * blocks : -1], refs[-1]
    total = None
    for delta in range(blocks):
        gated = gates[delta][...].astype(jnp.float32) * pieces[delta][...].astype(jnp.float32)
        total = gated * gated if total is None else total + gated * gated
    line = jnp.sum(jnp.transpose(total), axis=0, keepdims=True)
    for earlier in carried:
        line += earlier[...]
    out[...] = line


def make_squares(seq_index, query_gate, pieces, blocks, chunk, chunks, carried):
    tokens = query_gate.shape[0]
    return pl.pallas_call(
        functools.partial(squares_kernel, blocks),
        out_shape=jax.ShapeDtypeStruct((1, tokens), jnp.float32),
        grid_spec=pltpu.PrefetchScalarGridSpec(
            num_scalar_prefetch=1,
            grid=(1,),
            in_specs=[
                pl.BlockSpec((tokens, LANES), functools.partial(column_map, delta, chunk, chunks))
                for delta in range(blocks)
            ]
            + [pl.BlockSpec((tokens, LANES), lambda step, seq_ref: (0, 0))] * blocks
            + [pl.BlockSpec((1, tokens), lambda step, seq_ref: (0, 0))] * len(carried),
            out_specs=pl.BlockSpec((1, tokens), lambda step, seq_ref: (0, 0)),
        ),
        cost_estimate=pl.CostEstimate(
            flops=3 * tokens * LANES * blocks, bytes_accessed=4 * tokens * LANES * blocks, transcendentals=0
        ),
        compiler_params=pltpu.CompilerParams(vmem_limit_bytes=SMALL_BYTES),
    )(seq_index, *[query_gate] * blocks, *pieces, *carried)


def gate_kernel(blocks, chunk, chunks, seq_ref, *refs):
    gates, pieces = refs[:blocks], refs[blocks : 2 * blocks]
    out_ref, staged, sems = refs[-3:]
    copies = []
    for delta in range(blocks):
        gated = gates[delta][...].astype(jnp.float32) * pieces[delta][...].astype(jnp.float32)
        staged[delta] = gated.astype(jnp.bfloat16)
        place = pl.multiple_of(((seq_ref[0] ^ delta) * chunks + chunk) * LANES, LANES)
        copies.append(
            pltpu.make_async_copy(staged.at[delta], out_ref.at[:, pl.ds(place, LANES)], sems.at[delta])
        )
        copies[-1].start()
    for copy in copies:
        copy.wait()


def make_gate(seq_index, query_gate, pieces, blocks, chunk, chunks, so_far):
    tokens, channels = query_gate.shape
    return pl.pallas_call(
        functools.partial(gate_kernel, blocks, chunk, chunks),
        out_shape=jax.ShapeDtypeStruct((tokens, channels), jnp.bfloat16),
        grid_spec=pltpu.PrefetchScalarGridSpec(
            num_scalar_prefetch=1,
            grid=(1,),
            in_specs=[
                pl.BlockSpec((tokens, LANES), functools.partial(column_map, delta, chunk, chunks))
                for delta in range(blocks)
            ]
            + [pl.BlockSpec((tokens, LANES), lambda step, seq_ref: (0, 0))] * blocks
            + [ANYWHERE] * len(so_far),
            out_specs=ANYWHERE,
            scratch_shapes=[
                pltpu.VMEM((blocks, tokens, LANES), jnp.bfloat16),
                pltpu.SemaphoreType.DMA((blocks,)),
            ],
        ),
        input_output_aliases={2 * blocks + 1: 0} if so_far else {},
        cost_estimate=pl.CostEstimate(
            flops=tokens * LANES * blocks, bytes_accessed=6 * tokens * LANES * blocks, transcendentals=0
        ),
        compiler_params=pltpu.CompilerParams(vmem_limit_bytes=SMALL_BYTES),
    )(seq_index, *[query_gate] * blocks, *pieces, *so_far)


def finish_kernel(blocks, chunks, parts, seq_ref, gate_ref, gain_ref, *refs):
    sums, pieces, normed_ref = refs[:parts], refs[parts:-1], refs[-1]
    rows = gate_ref.shape[0]
    square_sum = sums[0][...]
    for part in sums[1:]:
        square_sum = square_sum + part[...]
    inverse = lax.rsqrt(square_sum / D + norm_eps)
    scale = jnp.transpose(jnp.broadcast_to(inverse, (LANES, rows)))
    for delta in range(blocks):
        for chunk in range(chunks):
            place = pl.multiple_of(((seq_ref[0] ^ delta) * chunks + chunk) * LANES, LANES)
            columns = pl.ds(place, LANES)
            piece = pieces[chunk * blocks + delta][...].astype(jnp.float32)
            gated = gate_ref[:, columns].astype(jnp.float32) * piece
            normed_ref[:, columns] = (gated * scale * gain_ref[:, columns]).astype(jnp.bfloat16)


def make_finish(seq_index, query_gate, norm_gain, sums, pieces, blocks, chunks):
    tokens, channels = query_gate.shape
    rows = FINISH_ROWS
    row_spec = pl.BlockSpec((rows, channels), lambda step, seq_ref: (step, 0))
    return pl.pallas_call(
        functools.partial(finish_kernel, blocks, chunks, len(sums)),
        out_shape=jax.ShapeDtypeStruct((tokens, channels), jnp.bfloat16),
        grid_spec=pltpu.PrefetchScalarGridSpec(
            num_scalar_prefetch=1,
            grid=(tokens // rows,),
            in_specs=[
                row_spec,
                pl.BlockSpec((1, channels), lambda step, seq_ref: (0, 0)),
            ]
            + [pl.BlockSpec((1, rows), lambda step, seq_ref: (0, step))] * len(sums)
            + [pl.BlockSpec((rows, LANES), lambda step, seq_ref: (step, 0))] * (blocks * chunks),
            out_specs=row_spec,
        ),
        cost_estimate=pl.CostEstimate(
            flops=4 * tokens * channels, bytes_accessed=8 * tokens * channels, transcendentals=tokens
        ),
        compiler_params=pltpu.CompilerParams(vmem_limit_bytes=SMALL_BYTES),
        name="finish",
    )(seq_index, query_gate, norm_gain[None, :], *sums, *pieces)


def exchange(pieces, blocks, turn):
    moved = {}
    for delta in ORDERS[turn]:
        moved[delta] = lax.ppermute(pieces[delta], "seq", pairs_of(blocks, delta))
    return [pieces[0]] + [moved[delta] for delta in range(1, blocks)]


def tiles_fit(tokens, channels, groups, blocks, width):
    if width & (width - 1) or blocks & (blocks - 1) or tokens != 2 * HALF or channels % (blocks * LANES):
        return False
    width_here, group_width = channels // blocks, channels // groups
    return LANES % group_width == 0 and width_here % group_width == 0


def body(query_gate, key_gate, value_input, filter_taps, norm_gain):
    tokens, channels = key_gate.shape
    blocks = lax.axis_size("seq")
    groups_here = filter_taps.shape[1]
    if not tiles_fit(tokens, channels, groups_here, blocks, lax.axis_size("chan")):
        return dense_body(query_gate, key_gate, value_input, filter_taps, norm_gain)
    chunks = channels // (blocks * LANES)
    groups = groups_here // blocks
    seq_index = lax.axis_index("seq").astype(jnp.int32)[None]
    taps = jnp.transpose(filter_taps)

    return tiled_body(
        seq_index, query_gate, key_gate, value_input, taps, norm_gain, blocks, groups, chunks
    )


def tiled_body(seq_index, query_gate, key_gate, value_input, taps, norm_gain, blocks, groups, chunks):
    tokens = key_gate.shape[0]
    received = []
    for chunk in range(chunks):
        sent = {}
        splits = (range(blocks // 2, blocks), range(blocks // 2)) if chunk == 0 else (range(blocks),)
        for turn, deltas in enumerate(splits):
            made = make_product(
                seq_index, key_gate, value_input, None if chunk else taps,
                blocks, tuple(deltas), chunk, chunks,
                FIRST_BYTES if chunk == 0 and turn == 0 else PRODUCT_BYTES,
            )
            sent.update(made)
        received.append(exchange(sent, blocks, chunk))
    returned = []
    after = []
    for chunk in range(chunks):
        local = make_conv(seq_index, received[chunk], received[0], blocks, tokens, groups, chunk, chunks, after)
        after = local[:1]
        returned.append(exchange(local, blocks, chunks + chunk))
    square_sum, gated = [], []
    for chunk in range(chunks):
        square_sum = [make_squares(seq_index, query_gate, returned[chunk], blocks, chunk, chunks, square_sum)]
        gated = [make_gate(seq_index, query_gate, returned[chunk], blocks, chunk, chunks, gated)]
    width = lax.axis_size("chan")
    sums = list(square_sum)
    for delta in range(width - 1, 0, -1):
        sums.append(lax.ppermute(square_sum[0], "chan", pairs_of(width, delta)))
    pieces = [piece for chunk in returned for piece in chunk]
    normed = make_finish(
        seq_index, query_gate, norm_gain, sums, pieces, blocks, chunks
    )
    return (gated[0], normed)


def solution(mesh):
    placed = (P("seq", "chan"), P("seq", "chan"), P("seq", "chan"), P("seq", "chan"), P("chan"))
    return jax.shard_map(
        body,
        mesh=mesh,
        in_specs=placed,
        out_specs=(P("seq", "chan"), P("seq", "chan")),
        check_vma=False,
    )
```

profile of v0, /device:TPU:0, one launch (start us, length us, event | category | flops | bytes accessed | tf_op | source)
XLA Modules:
  0.0 126.5 jit_solution(11348583330773514894)
XLA Ops:
  0.6 2.3 %shard_map.69 = (bf16[528,128]{1,0:T(8,128)(2,1)}, bf16[528,128]{1,0:T(8,128)(2,1)}, bf16[528,128]{1,0:T(8,128)(2,1)}, bf16[528,128]{1,0:T(8,128)(2,1)}) custom-call(s32[1]{0:T(128)} %bitcast.seq_ref, bf16[512,2048]{1,0:T(8,128)(2,1)} %refs_3_.9, bf16[512,2048]{1,0:T(8,128)(2,1)} %refs_3_.9, bf16[512,2048]{1,0:T(8,128)(2,1)} %refs_3_.9, ...), custom_call_target="tpu_custom_call" | custom-call | flops 262144 | bytes 1572864 | tf_op jit(solution)/shard_map/pallas_call | solution.py:174
  2.9 3.0 %collective-permute-start.7 = (bf16[528,128]{1,0:T(8,128)(2,1)}, bf16[528,128]{1,0:T(8,128)(2,1)S(1)}, u32[]{:S(2)}, u32[]{:S(2)}) collective-permute-start(bf16[528,128]{1,0:T(8,128)(2,1)} %get-tuple-element.43), channel_id=1, source_target_pairs={{0,4},{4,0},{8,12},{12,8},{16,20},{20,16},{24,28},{28,24},{1,5},{5... | collective-permute-start | bytes 405512 | tf_op jit(solution)/shard_map/ppermute | solution.py:407
  5.9 1.6 %collective-permute-start.8 = (bf16[528,128]{1,0:T(8,128)(2,1)}, bf16[528,128]{1,0:T(8,128)(2,1)S(1)}, u32[]{:S(2)}, u32[]{:S(2)}) collective-permute-start(bf16[528,128]{1,0:T(8,128)(2,1)} %get-tuple-element.44), channel_id=1, source_target_pairs={{0,8},{4,12},{8,0},{12,4},{16,24},{20,28},{24,16},{28,20},{1,9},{5... | collective-permute-start | bytes 405512 | tf_op jit(solution)/shard_map/ppermute | solution.py:407
  7.5 2.7 %shard_map.68 = (bf16[512,128]{1,0:T(8,128)(2,1)}, bf16[512,128]{1,0:T(8,128)(2,1)}, bf16[512,128]{1,0:T(8,128)(2,1)}, bf16[512,128]{1,0:T(8,128)(2,1)}, bf16[51...) custom-call(s32[1]{0:T(128)} %bitcast.seq_ref, ...), custom_call_target="tpu_custom_call" | custom-call | flops 524288 | bytes 3145728 | tf_op jit(solution)/shard_map/pallas_call | solution.py:174
  10.2 0.5 collective-permute-start
  10.7 0.0 collective-permute-start.1
  10.8 0.0 copy-start.2
  10.8 3.0 %collective-permute-start.9 = (bf16[528,128]{1,0:T(8,128)(2,1)S(1)}, bf16[528,128]{1,0:T(8,128)(2,1)S(1)}, u32[]{:S(2)}, u32[]{:S(2)}) collective-permute-start(bf16[528,128]{1,0:T(8,128)(2,1)S(1)} %copy-done.4), channel_id=1, source_target_pairs={{0,12},{4,8},{8,4},{12,0},{16,28},{20,24},{24,20},{28,16},{1,13},{... | collective-permute-start | bytes 405512 | tf_op jit(solution)/shard_map/ppermute | solution.py:407
  13.8 2.3 %shard_map.70 = (bf16[528,128]{1,0:T(8,128)(2,1)}, bf16[528,128]{1,0:T(8,128)(2,1)}, bf16[528,128]{1,0:T(8,128)(2,1)}, bf16[528,128]{1,0:T(8,128)(2,1)}) custom-call(s32[1]{0:T(128)} %bitcast.seq_ref, bf16[512,2048]{1,0:T(8,128)(2,1)} %refs_3_.9, bf16[512,2048]{1,0:T(8,128)(2,1)} %refs_3_.9, bf16[512,2048]{1,0:T(8,128)(2,1)} %refs_3_.9, ...), custom_call_target="tpu_custom_call" | custom-call | flops 262144 | bytes 1572864 | tf_op jit(solution)/shard_map/pallas_call | solution.py:174
  16.1 0.4 collective-permute-done.refs_1_
  16.4 2.6 %collective-permute-start.10 = (bf16[528,128]{1,0:T(8,128)(2,1)}, bf16[528,128]{1,0:T(8,128)(2,1)S(1)}, u32[]{:S(2)}, u32[]{:S(2)}) collective-permute-start(bf16[528,128]{1,0:T(8,128)(2,1)} %get-tuple-element.46), channel_id=1, source_target_pairs={{0,16},{4,20},{8,24},{12,28},{16,0},{20,4},{24,8},{28,12},{1,17},{... | collective-permute-start | bytes 405512 | tf_op jit(solution)/shard_map/ppermute | solution.py:407
  19.0 1.8 %collective-permute-start.11 = (bf16[528,128]{1,0:T(8,128)(2,1)}, bf16[528,128]{1,0:T(8,128)(2,1)S(1)}, u32[]{:S(2)}, u32[]{:S(2)}) collective-permute-start(bf16[528,128]{1,0:T(8,128)(2,1)} %get-tuple-element.47), channel_id=1, source_target_pairs={{0,20},{4,16},{8,28},{12,24},{16,4},{20,0},{24,12},{28,8},{1,21},{... | collective-permute-start | bytes 405512 | tf_op jit(solution)/shard_map/ppermute | solution.py:407
  20.8 0.7 collective-permute-start.12
  21.5 3.1 %collective-permute-start.13 = (bf16[528,128]{1,0:T(8,128)(2,1)}, bf16[528,128]{1,0:T(8,128)(2,1)S(1)}, u32[]{:S(2)}, u32[]{:S(2)}) collective-permute-start(bf16[528,128]{1,0:T(8,128)(2,1)} %get-tuple-element.49), channel_id=1, source_target_pairs={{0,28},{4,24},{8,20},{12,16},{16,12},{20,8},{24,4},{28,0},{1,29},{... | collective-permute-start | bytes 405512 | tf_op jit(solution)/shard_map/ppermute | solution.py:407
  24.6 10.7 %collective-permute-done.10.refs_4_.refs_12_ = bf16[528,128]{1,0:T(8,128)(2,1)S(1)} collective-permute-done((bf16[528,128]{1,0:T(8,128)(2,1)}, bf16[528,128]{1,0:T(8,128)(2,1)S(1)}, u32[]{:S(2)}, u32[]{:S(2)}) %collective-permute-start.10) | collective-permute-done | bytes 135200 | tf_op jit(solution)/shard_map/ppermute | solution.py:407
  35.3 3.5 %collective-permute-done.11.refs_5_.refs_13_ = bf16[528,128]{1,0:T(8,128)(2,1)S(1)} collective-permute-done((bf16[528,128]{1,0:T(8,128)(2,1)}, bf16[528,128]{1,0:T(8,128)(2,1)S(1)}, u32[]{:S(2)}, u32[]{:S(2)}) %collective-permute-start.11) | collective-permute-done | bytes 135200 | tf_op jit(solution)/shard_map/ppermute | solution.py:407
  38.8 1.9 %collective-permute-start.5 = (bf16[512,128]{1,0:T(8,128)(2,1)S(1)}, bf16[512,128]{1,0:T(8,128)(2,1)S(1)}, u32[]{:S(2)}, u32[]{:S(2)}) collective-permute-start(bf16[512,128]{1,0:T(8,128)(2,1)S(1)} %copy-done.6), channel_id=1, source_target_pairs={{0,24},{4,28},{8,16},{12,20},{16,8},{20,12},{24,0},{28,4},{1,25},{... | collective-permute-start | bytes 393224 | tf_op jit(solution)/shard_map/ppermute | solution.py:407
  40.7 2.6 %collective-permute-start.6 = (bf16[512,128]{1,0:T(8,128)(2,1)S(1)}, bf16[512,128]{1,0:T(8,128)(2,1)S(1)}, u32[]{:S(2)}, u32[]{:S(2)}) collective-permute-start(bf16[512,128]{1,0:T(8,128)(2,1)S(1)} %copy-done.5), channel_id=1, source_target_pairs={{0,28},{4,24},{8,20},{12,16},{16,12},{20,8},{24,4},{28,0},{1,29},{... | collective-permute-start | bytes 393224 | tf_op jit(solution)/shard_map/ppermute | solution.py:407
  43.3 5.3 %shard_map.71 = (bf16[512,128]{1,0:T(8,128)(2,1)S(1)}, bf16[512,128]{1,0:T(8,128)(2,1)S(1)}, bf16[512,128]{1,0:T(8,128)(2,1)S(1)}, bf16[512,128]{1,0:T(8,128)(2,...) custom-call(s32[1]{0:T(128)} %bitcast.seq_ref, ...), custom_call_target="tpu_custom_call" | custom-call | flops 9663676416 | bytes 2097152 | tf_op jit(solution)/shard_map/pallas_call | solution.py:258
  48.6 8.3 %collective-permute-done.3.refs_4_ = bf16[512,128]{1,0:T(8,128)(2,1)S(1)} collective-permute-done((bf16[512,128]{1,0:T(8,128)(2,1)S(1)}, bf16[512,128]{1,0:T(8,128)(2,1)S(1)}, u32[]{:S(2)}, u32[]{:S(2)}) %collective-permute-start.3) | collective-permute-done | bytes 131104 | tf_op jit(solution)/shard_map/ppermute | solution.py:407
  57.0 3.1 %collective-permute-done.4.refs_5_ = bf16[512,128]{1,0:T(8,128)(2,1)S(1)} collective-permute-done((bf16[512,128]{1,0:T(8,128)(2,1)S(1)}, bf16[512,128]{1,0:T(8,128)(2,1)S(1)}, u32[]{:S(2)}, u32[]{:S(2)}) %collective-permute-start.4) | collective-permute-done | bytes 131104 | tf_op jit(solution)/shard_map/ppermute | solution.py:407
  60.0 0.0 copy-start
  60.1 5.3 %shard_map.72 = (bf16[512,128]{1,0:T(8,128)(2,1)S(1)}, bf16[512,128]{1,0:T(8,128)(2,1)S(1)}, bf16[512,128]{1,0:T(8,128)(2,1)S(1)}, bf16[512,128]{1,0:T(8,128)(2,...) custom-call(s32[1]{0:T(128)} %bitcast.seq_ref, ...), custom_call_target="tpu_custom_call" | custom-call | flops 9663676416 | bytes 2097152 | tf_op jit(solution)/shard_map/pallas_call | solution.py:258
  65.3 1.3 collective-permute-start.14
  66.6 4.7 %collective-permute-start.15 = (bf16[512,128]{1,0:T(8,128)(2,1)S(1)}, bf16[512,128]{1,0:T(8,128)(2,1)S(1)}, u32[]{:S(2)}, u32[]{:S(2)}) collective-permute-start(bf16[512,128]{1,0:T(8,128)(2,1)S(1)} %get-tuple-element.53), channel_id=1, source_target_pairs={{0,8},{4,12},{8,0},{12,4},{16,24},{20,28},{24,16},{28,20},{1,9},{5... | collective-permute-start | bytes 393224 | tf_op jit(solution)/shard_map/ppermute | solution.py:407
  71.3 1.0 collective-permute-start.21
  72.3 2.5 %collective-permute-start.23 = (bf16[512,128]{1,0:T(8,128)(2,1)S(1)}, bf16[512,128]{1,0:T(8,128)(2,1)S(1)}, u32[]{:S(2)}, u32[]{:S(2)}) collective-permute-start(bf16[512,128]{1,0:T(8,128)(2,1)S(1)} %get-tuple-element.61), channel_id=1, source_target_pairs={{0,12},{4,8},{8,4},{12,0},{16,28},{20,24},{24,20},{28,16},{1,13},{... | collective-permute-start | bytes 393224 | tf_op jit(solution)/shard_map/ppermute | solution.py:407
  74.8 2.0 %collective-permute-start.24 = (bf16[512,128]{1,0:T(8,128)(2,1)S(1)}, bf16[512,128]{1,0:T(8,128)(2,1)S(1)}, u32[]{:S(2)}, u32[]{:S(2)}) collective-permute-start(bf16[512,128]{1,0:T(8,128)(2,1)S(1)} %get-tuple-element.62), channel_id=1, source_target_pairs={{0,16},{4,20},{8,24},{12,28},{16,0},{20,4},{24,8},{28,12},{1,17},{... | collective-permute-start | bytes 393224 | tf_op jit(solution)/shard_map/ppermute | solution.py:407
  76.8 0.2 collective-permute-done.15.refs_10_.refs_14_
  77.0 1.7 %collective-permute-start.25 = (bf16[512,128]{1,0:T(8,128)(2,1)S(1)}, bf16[512,128]{1,0:T(8,128)(2,1)S(1)}, u32[]{:S(2)}, u32[]{:S(2)}) collective-permute-start(bf16[512,128]{1,0:T(8,128)(2,1)S(1)} %get-tuple-element.63), channel_id=1, source_target_pairs={{0,20},{4,16},{8,28},{12,24},{16,4},{20,0},{24,12},{28,8},{1,21},{... | collective-permute-start | bytes 393224 | tf_op jit(solution)/shard_map/ppermute | solution.py:407
  78.7 1.7 %collective-permute-start.26 = (bf16[512,128]{1,0:T(8,128)(2,1)S(1)}, bf16[512,128]{1,0:T(8,128)(2,1)S(1)}, u32[]{:S(2)}, u32[]{:S(2)}) collective-permute-start(bf16[512,128]{1,0:T(8,128)(2,1)S(1)} %get-tuple-element.64), channel_id=1, source_target_pairs={{0,24},{4,28},{8,16},{12,20},{16,8},{20,12},{24,0},{28,4},{1,25},{... | collective-permute-start | bytes 393224 | tf_op jit(solution)/shard_map/ppermute | solution.py:407
  80.5 1.4 %collective-permute-done.22.refs_10_.refs_6_ = bf16[512,128]{1,0:T(8,128)(2,1)S(1)} collective-permute-done((bf16[512,128]{1,0:T(8,128)(2,1)S(1)}, bf16[512,128]{1,0:T(8,128)(2,1)S(1)}, u32[]{:S(2)}, u32[]{:S(2)}) %collective-permute-start.22) | collective-permute-done | bytes 131104 | tf_op jit(solution)/shard_map/ppermute | solution.py:407
  81.9 2.6 %collective-permute-start.27 = (bf16[512,128]{1,0:T(8,128)(2,1)S(1)}, bf16[512,128]{1,0:T(8,128)(2,1)S(1)}, u32[]{:S(2)}, u32[]{:S(2)}) collective-permute-start(bf16[512,128]{1,0:T(8,128)(2,1)S(1)} %get-tuple-element.65), channel_id=1, source_target_pairs={{0,28},{4,24},{8,20},{12,16},{16,12},{20,8},{24,4},{28,0},{1,29},{... | collective-permute-start | bytes 393224 | tf_op jit(solution)/shard_map/ppermute | solution.py:407
  84.5 7.1 %collective-permute-done.24.refs_12_.refs_8_ = bf16[512,128]{1,0:T(8,128)(2,1)S(1)} collective-permute-done((bf16[512,128]{1,0:T(8,128)(2,1)S(1)}, bf16[512,128]{1,0:T(8,128)(2,1)S(1)}, u32[]{:S(2)}, u32[]{:S(2)}) %collective-permute-start.24) | collective-permute-done | bytes 131104 | tf_op jit(solution)/shard_map/ppermute | solution.py:407
  91.6 11.9 %collective-permute-done.25.refs_13_.refs_9_ = bf16[512,128]{1,0:T(8,128)(2,1)S(1)} collective-permute-done((bf16[512,128]{1,0:T(8,128)(2,1)S(1)}, bf16[512,128]{1,0:T(8,128)(2,1)S(1)}, u32[]{:S(2)}, u32[]{:S(2)}) %collective-permute-start.25) | collective-permute-done | bytes 131104 | tf_op jit(solution)/shard_map/ppermute | solution.py:407
  103.5 1.7 %collective-permute-start.19 = (bf16[512,128]{1,0:T(8,128)(2,1)S(1)}, bf16[512,128]{1,0:T(8,128)(2,1)S(1)}, u32[]{:S(2)}, u32[]{:S(2)}) collective-permute-start(bf16[512,128]{1,0:T(8,128)(2,1)S(1)} %get-tuple-element.57), channel_id=1, source_target_pairs={{0,24},{4,28},{8,16},{12,20},{16,8},{20,12},{24,0},{28,4},{1,25},{... | collective-permute-start | bytes 393224 | tf_op jit(solution)/shard_map/ppermute | solution.py:407
  105.2 2.7 %collective-permute-start.20 = (bf16[512,128]{1,0:T(8,128)(2,1)S(1)}, bf16[512,128]{1,0:T(8,128)(2,1)S(1)}, u32[]{:S(2)}, u32[]{:S(2)}) collective-permute-start(bf16[512,128]{1,0:T(8,128)(2,1)S(1)} %get-tuple-element.58), channel_id=1, source_target_pairs={{0,28},{4,24},{8,20},{12,16},{16,12},{20,8},{24,4},{28,0},{1,29},{... | collective-permute-start | bytes 393224 | tf_op jit(solution)/shard_map/ppermute | solution.py:407
  107.9 0.5 shard_map.75.refs_16_
  108.5 7.3 %collective-permute-done.17.refs_12_.refs_16_ = bf16[512,128]{1,0:T(8,128)(2,1)S(1)} collective-permute-done((bf16[512,128]{1,0:T(8,128)(2,1)S(1)}, bf16[512,128]{1,0:T(8,128)(2,1)S(1)}, u32[]{:S(2)}, u32[]{:S(2)}) %collective-permute-start.17) | collective-permute-done | bytes 131104 | tf_op jit(solution)/shard_map/ppermute | solution.py:407
  115.8 2.9 %collective-permute-done.18.refs_13_.refs_17_ = bf16[512,128]{1,0:T(8,128)(2,1)S(1)} collective-permute-done((bf16[512,128]{1,0:T(8,128)(2,1)S(1)}, bf16[512,128]{1,0:T(8,128)(2,1)S(1)}, u32[]{:S(2)}, u32[]{:S(2)}) %collective-permute-start.18) | collective-permute-done | bytes 131104 | tf_op jit(solution)/shard_map/ppermute | solution.py:407
  118.7 0.7 shard_map.76.refs_0_
  119.4 0.1 collective-permute-start.28
  119.5 1.6 %collective-permute-start.29 = (f32[1,512]{1,0:T(1,128)S(1)}, f32[1,512]{1,0:T(1,128)S(1)}, u32[]{:S(2)}, u32[]{:S(2)}) collective-permute-start(f32[1,512]{1,0:T(1,128)S(1)} %shard_map.76.refs_0_), channel_id=1, source_target_pairs={{0,2},{1,3},{2,0},{3,1},{4,6},{5,7},{6,4},{7,5},{8,10},{9,11},{10,... | collective-permute-start | bytes 6152 | tf_op jit(solution)/shard_map/ppermute | solution.py:461
  121.1 0.3 collective-permute-start.30
  121.3 1.3 %shard_map.73.refs_16_ = bf16[512,2048]{1,0:T(8,128)(2,1)} custom-call(s32[1]{0:T(128)} %bitcast.seq_ref, bf16[512,2048]{1,0:T(8,128)(2,1)S(1)} %copy-done, bf16[512,2048]{1,0:T(8,128)(2,1)S(1)} %copy-done, bf16[512,2048]{1,0:T(8,128)(2,1)S(1)} %copy-done, bf16[512,2048]{1,0:T(8,128)(2,1)S(1)} %copy-done, bf16[512,2048]{1,0:T(8,128)(2,1)S(1)} %copy-done, ...), custom_call_target="tpu_custom_call" | custom-call | flops 524288 | bytes 3145728 | tf_op jit(solution)/shard_map/pallas_call | solution.py:335
  122.7 0.0 copy-start.1
  122.7 1.4 %shard_map.74 = bf16[512,2048]{1,0:T(8,128)(2,1)} custom-call(s32[1]{0:T(128)} %bitcast.seq_ref, bf16[512,2048]{1,0:T(8,128)(2,1)S(1)} %copy-done, bf16[512,2048]{1,0:T(8,128)(2,1)S(1)} %copy-done, bf16[512,2048]{1,0:T(8,128)(2,1)S(1)} %copy-done, bf16[512,2048]{1,0:T(8,128)(2,1)S(1)} %copy-done, ...), custom_call_target="tpu_custom_call", output_to_operand_aliasing={{}: (17, {})} | custom-call | flops 524288 | bytes 3145728 | tf_op jit(solution)/shard_map/pallas_call | solution.py:335
  124.1 2.4 %finish.1 = bf16[512,2048]{1,0:T(8,128)(2,1)} custom-call(s32[1]{0:T(128)} %bitcast.seq_ref, bf16[512,2048]{1,0:T(8,128)(2,1)S(1)} %copy-done, f32[1,2048]{1,0:T(1,128)S(1)} %bitcast.3, f32[1,512]{1,0:T(1,128)S(1)} %shard_map.76.refs_0_, f32[1,512]{1,0:T(1,128)S(1)} %collective-permute-done.28.refs_1_, f32[1,512]{1,0:T(1,128)S(1)} %collective-permute-done.29.refs_2_, ...), custom_call_target="tpu_custom_call" | custom-call | flops 4194304 | bytes 8388608 | tf_op jit(solution)/shard_map/finish/pallas_call | solution.py:382
  (44 shorter events, 0.1 us)
Async XLA Ops:
  2.9 17.9 %collective-permute-start.7 = (bf16[528,128]{1,0:T(8,128)(2,1)}, bf16[528,128]{1,0:T(8,128)(2,1)S(1)}, u32[]{:S(2)}, u32[]{:S(2)}) collective-permute-start(bf16[528,128]{1,0:T(8,128)(2,1)} %get-tuple-element.43), channel_id=1, source_target_pairs={{0,4},{4,0},{8,12},{12,8},{16,20},{20,16},{24,28},{28,24},{1,5},{5... | collective-permute-start | bytes 405512 | tf_op jit(solution)/shard_map/ppermute | solution.py:407
  5.9 4.9 %copy-start.4 = (bf16[528,128]{1,0:T(8,128)(2,1)S(1)}, bf16[528,128]{1,0:T(8,128)(2,1)}, u32[]{:S(2)}) copy-start(bf16[528,128]{1,0:T(8,128)(2,1)} %get-tuple-element.45) | copy-start | bytes 405508
  5.9 15.6 %collective-permute-start.8 = (bf16[528,128]{1,0:T(8,128)(2,1)}, bf16[528,128]{1,0:T(8,128)(2,1)S(1)}, u32[]{:S(2)}, u32[]{:S(2)}) collective-permute-start(bf16[528,128]{1,0:T(8,128)(2,1)} %get-tuple-element.44), channel_id=1, source_target_pairs={{0,8},{4,12},{8,0},{12,4},{16,24},{20,28},{24,16},{28,20},{1,9},{5... | collective-permute-start | bytes 405512 | tf_op jit(solution)/shard_map/ppermute | solution.py:407
  10.2 6.3 %collective-permute-start = (bf16[512,128]{1,0:T(8,128)(2,1)}, bf16[512,128]{1,0:T(8,128)(2,1)S(1)}, u32[]{:S(2)}, u32[]{:S(2)}) collective-permute-start(bf16[512,128]{1,0:T(8,128)(2,1)} %get-tuple-element.35), channel_id=1, source_target_pairs={{0,4},{4,0},{8,12},{12,8},{16,20},{20,16},{24,28},{28,24},{1,5},{5... | collective-permute-start | bytes 393224 | tf_op jit(solution)/shard_map/ppermute | solution.py:407
  10.7 8.3 %collective-permute-start.1 = (bf16[512,128]{1,0:T(8,128)(2,1)}, bf16[512,128]{1,0:T(8,128)(2,1)S(1)}, u32[]{:S(2)}, u32[]{:S(2)}) collective-permute-start(bf16[512,128]{1,0:T(8,128)(2,1)} %get-tuple-element.36), channel_id=1, source_target_pairs={{0,8},{4,12},{8,0},{12,4},{16,24},{20,28},{24,16},{28,20},{1,9},{5... | collective-permute-start | bytes 393224 | tf_op jit(solution)/shard_map/ppermute | solution.py:407
  10.8 13.9 %copy-start.9 = (bf16[512,128]{1,0:T(8,128)(2,1)S(1)}, bf16[512,128]{1,0:T(8,128)(2,1)}, u32[]{:S(2)}) copy-start(bf16[512,128]{1,0:T(8,128)(2,1)} %get-tuple-element.37) | copy-start | bytes 393220
  10.8 24.5 %copy-start.8 = (bf16[512,128]{1,0:T(8,128)(2,1)S(1)}, bf16[512,128]{1,0:T(8,128)(2,1)}, u32[]{:S(2)}) copy-start(bf16[512,128]{1,0:T(8,128)(2,1)} %get-tuple-element.38) | copy-start | bytes 393220
  10.8 28.0 %copy-start.7 = (bf16[512,128]{1,0:T(8,128)(2,1)S(1)}, bf16[512,128]{1,0:T(8,128)(2,1)}, u32[]{:S(2)}) copy-start(bf16[512,128]{1,0:T(8,128)(2,1)} %get-tuple-element.39) | copy-start | bytes 393220
  10.8 28.0 %copy-start.6 = (bf16[512,128]{1,0:T(8,128)(2,1)S(1)}, bf16[512,128]{1,0:T(8,128)(2,1)}, u32[]{:S(2)}) copy-start(bf16[512,128]{1,0:T(8,128)(2,1)} %get-tuple-element.40) | copy-start | bytes 393220
  10.8 30.0 %copy-start.5 = (bf16[512,128]{1,0:T(8,128)(2,1)S(1)}, bf16[512,128]{1,0:T(8,128)(2,1)}, u32[]{:S(2)}) copy-start(bf16[512,128]{1,0:T(8,128)(2,1)} %get-tuple-element.41) | copy-start | bytes 393220
  10.8 32.6 %copy-start.2 = (bf16[528,128]{1,0:T(8,128)(2,1)S(1)}, bf16[528,128]{1,0:T(8,128)(2,1)}, u32[]{:S(2)}) copy-start(bf16[528,128]{1,0:T(8,128)(2,1)} %get-tuple-element.42.refs_0_.refs_8_) | copy-start | bytes 405508
  10.8 13.8 %collective-permute-start.9 = (bf16[528,128]{1,0:T(8,128)(2,1)S(1)}, bf16[528,128]{1,0:T(8,128)(2,1)S(1)}, u32[]{:S(2)}, u32[]{:S(2)}) collective-permute-start(bf16[528,128]{1,0:T(8,128)(2,1)S(1)} %copy-done.4), channel_id=1, source_target_pairs={{0,12},{4,8},{8,4},{12,0},{16,28},{20,24},{24,20},{28,16},{1,13},{... | collective-permute-start | bytes 405512 | tf_op jit(solution)/shard_map/ppermute | solution.py:407
  16.4 18.9 %collective-permute-start.10 = (bf16[528,128]{1,0:T(8,128)(2,1)}, bf16[528,128]{1,0:T(8,128)(2,1)S(1)}, u32[]{:S(2)}, u32[]{:S(2)}) collective-permute-start(bf16[528,128]{1,0:T(8,128)(2,1)} %get-tuple-element.46), channel_id=1, source_target_pairs={{0,16},{4,20},{8,24},{12,28},{16,0},{20,4},{24,8},{28,12},{1,17},{... | collective-permute-start | bytes 405512 | tf_op jit(solution)/shard_map/ppermute | solution.py:407
  19.0 19.7 %collective-permute-start.11 = (bf16[528,128]{1,0:T(8,128)(2,1)}, bf16[528,128]{1,0:T(8,128)(2,1)S(1)}, u32[]{:S(2)}, u32[]{:S(2)}) collective-permute-start(bf16[528,128]{1,0:T(8,128)(2,1)} %get-tuple-element.47), channel_id=1, source_target_pairs={{0,20},{4,16},{8,28},{12,24},{16,4},{20,0},{24,12},{28,8},{1,21},{... | collective-permute-start | bytes 405512 | tf_op jit(solution)/shard_map/ppermute | solution.py:407
  20.8 18.0 %collective-permute-start.12 = (bf16[528,128]{1,0:T(8,128)(2,1)}, bf16[528,128]{1,0:T(8,128)(2,1)S(1)}, u32[]{:S(2)}, u32[]{:S(2)}) collective-permute-start(bf16[528,128]{1,0:T(8,128)(2,1)} %get-tuple-element.48), channel_id=1, source_target_pairs={{0,24},{4,28},{8,16},{12,20},{16,8},{20,12},{24,0},{28,4},{1,25},{... | collective-permute-start | bytes 405512 | tf_op jit(solution)/shard_map/ppermute | solution.py:407
  21.5 19.2 %collective-permute-start.13 = (bf16[528,128]{1,0:T(8,128)(2,1)}, bf16[528,128]{1,0:T(8,128)(2,1)S(1)}, u32[]{:S(2)}, u32[]{:S(2)}) collective-permute-start(bf16[528,128]{1,0:T(8,128)(2,1)} %get-tuple-element.49), channel_id=1, source_target_pairs={{0,28},{4,24},{8,20},{12,16},{16,12},{20,8},{24,4},{28,0},{1,29},{... | collective-permute-start | bytes 405512 | tf_op jit(solution)/shard_map/ppermute | solution.py:407
  24.6 24.0 %collective-permute-start.2 = (bf16[512,128]{1,0:T(8,128)(2,1)S(1)}, bf16[512,128]{1,0:T(8,128)(2,1)S(1)}, u32[]{:S(2)}, u32[]{:S(2)}) collective-permute-start(bf16[512,128]{1,0:T(8,128)(2,1)S(1)} %copy-done.9), channel_id=1, source_target_pairs={{0,12},{4,8},{8,4},{12,0},{16,28},{20,24},{24,20},{28,16},{1,13},{... | collective-permute-start | bytes 393224 | tf_op jit(solution)/shard_map/ppermute | solution.py:407
  35.3 21.6 %collective-permute-start.3 = (bf16[512,128]{1,0:T(8,128)(2,1)S(1)}, bf16[512,128]{1,0:T(8,128)(2,1)S(1)}, u32[]{:S(2)}, u32[]{:S(2)}) collective-permute-start(bf16[512,128]{1,0:T(8,128)(2,1)S(1)} %copy-done.8), channel_id=1, source_target_pairs={{0,16},{4,20},{8,24},{12,28},{16,0},{20,4},{24,8},{28,12},{1,17},{... | collective-permute-start | bytes 393224 | tf_op jit(solution)/shard_map/ppermute | solution.py:407
  38.8 21.2 %collective-permute-start.4 = (bf16[512,128]{1,0:T(8,128)(2,1)S(1)}, bf16[512,128]{1,0:T(8,128)(2,1)S(1)}, u32[]{:S(2)}, u32[]{:S(2)}) collective-permute-start(bf16[512,128]{1,0:T(8,128)(2,1)S(1)} %copy-done.7), channel_id=1, source_target_pairs={{0,20},{4,16},{8,28},{12,24},{16,4},{20,0},{24,12},{28,8},{1,21},{... | collective-permute-start | bytes 393224 | tf_op jit(solution)/shard_map/ppermute | solution.py:407
  38.8 21.2 %collective-permute-start.5 = (bf16[512,128]{1,0:T(8,128)(2,1)S(1)}, bf16[512,128]{1,0:T(8,128)(2,1)S(1)}, u32[]{:S(2)}, u32[]{:S(2)}) collective-permute-start(bf16[512,128]{1,0:T(8,128)(2,1)S(1)} %copy-done.6), channel_id=1, source_target_pairs={{0,24},{4,28},{8,16},{12,20},{16,8},{20,12},{24,0},{28,4},{1,25},{... | collective-permute-start | bytes 393224 | tf_op jit(solution)/shard_map/ppermute | solution.py:407
  40.7 19.3 %collective-permute-start.6 = (bf16[512,128]{1,0:T(8,128)(2,1)S(1)}, bf16[512,128]{1,0:T(8,128)(2,1)S(1)}, u32[]{:S(2)}, u32[]{:S(2)}) collective-permute-start(bf16[512,128]{1,0:T(8,128)(2,1)S(1)} %copy-done.5), channel_id=1, source_target_pairs={{0,28},{4,24},{8,20},{12,16},{16,12},{20,8},{24,4},{28,0},{1,29},{... | collective-permute-start | bytes 393224 | tf_op jit(solution)/shard_map/ppermute | solution.py:407
  43.3 16.7 %copy-start.3 = (bf16[512,128]{1,0:T(8,128)(2,1)S(1)}, bf16[512,128]{1,0:T(8,128)(2,1)}, u32[]{:S(2)}) copy-start(bf16[512,128]{1,0:T(8,128)(2,1)} %get-tuple-element.34.refs_0_) | copy-start | bytes 393220
  60.0 47.9 %copy-start = (bf16[512,2048]{1,0:T(8,128)(2,1)S(1)}, bf16[512,2048]{1,0:T(8,128)(2,1)}, u32[]{:S(2)}) copy-start(bf16[512,2048]{1,0:T(8,128)(2,1)} %gate_ref.1) | copy-start | bytes 6291460
  65.3 9.5 %collective-permute-start.14 = (bf16[512,128]{1,0:T(8,128)(2,1)S(1)}, bf16[512,128]{1,0:T(8,128)(2,1)S(1)}, u32[]{:S(2)}, u32[]{:S(2)}) collective-permute-start(bf16[512,128]{1,0:T(8,128)(2,1)S(1)} %get-tuple-element.52), channel_id=1, source_target_pairs={{0,4},{4,0},{8,12},{12,8},{16,20},{20,16},{24,28},{28,24},{1,5},{5... | collective-permute-start | bytes 393224 | tf_op jit(solution)/shard_map/ppermute | solution.py:407
  66.6 10.4 %collective-permute-start.15 = (bf16[512,128]{1,0:T(8,128)(2,1)S(1)}, bf16[512,128]{1,0:T(8,128)(2,1)S(1)}, u32[]{:S(2)}, u32[]{:S(2)}) collective-permute-start(bf16[512,128]{1,0:T(8,128)(2,1)S(1)} %get-tuple-element.53), channel_id=1, source_target_pairs={{0,8},{4,12},{8,0},{12,4},{16,24},{20,28},{24,16},{28,20},{1,9},{5... | collective-permute-start | bytes 393224 | tf_op jit(solution)/shard_map/ppermute | solution.py:407
  71.3 7.4 %collective-permute-start.21 = (bf16[512,128]{1,0:T(8,128)(2,1)S(1)}, bf16[512,128]{1,0:T(8,128)(2,1)S(1)}, u32[]{:S(2)}, u32[]{:S(2)}) collective-permute-start(bf16[512,128]{1,0:T(8,128)(2,1)S(1)} %get-tuple-element.59), channel_id=1, source_target_pairs={{0,4},{4,0},{8,12},{12,8},{16,20},{20,16},{24,28},{28,24},{1,5},{5... | collective-permute-start | bytes 393224 | tf_op jit(solution)/shard_map/ppermute | solution.py:407
  72.3 9.6 %collective-permute-start.22 = (bf16[512,128]{1,0:T(8,128)(2,1)S(1)}, bf16[512,128]{1,0:T(8,128)(2,1)S(1)}, u32[]{:S(2)}, u32[]{:S(2)}) collective-permute-start(bf16[512,128]{1,0:T(8,128)(2,1)S(1)} %get-tuple-element.60), channel_id=1, source_target_pairs={{0,8},{4,12},{8,0},{12,4},{16,24},{20,28},{24,16},{28,20},{1,9},{5... | collective-permute-start | bytes 393224 | tf_op jit(solution)/shard_map/ppermute | solution.py:407
  72.3 12.2 %collective-permute-start.23 = (bf16[512,128]{1,0:T(8,128)(2,1)S(1)}, bf16[512,128]{1,0:T(8,128)(2,1)S(1)}, u32[]{:S(2)}, u32[]{:S(2)}) collective-permute-start(bf16[512,128]{1,0:T(8,128)(2,1)S(1)} %get-tuple-element.61), channel_id=1, source_target_pairs={{0,12},{4,8},{8,4},{12,0},{16,28},{20,24},{24,20},{28,16},{1,13},{... | collective-permute-start | bytes 393224 | tf_op jit(solution)/shard_map/ppermute | solution.py:407
  74.8 16.8 %collective-permute-start.24 = (bf16[512,128]{1,0:T(8,128)(2,1)S(1)}, bf16[512,128]{1,0:T(8,128)(2,1)S(1)}, u32[]{:S(2)}, u32[]{:S(2)}) collective-permute-start(bf16[512,128]{1,0:T(8,128)(2,1)S(1)} %get-tuple-element.62), channel_id=1, source_target_pairs={{0,16},{4,20},{8,24},{12,28},{16,0},{20,4},{24,8},{28,12},{1,17},{... | collective-permute-start | bytes 393224 | tf_op jit(solution)/shard_map/ppermute | solution.py:407
  77.0 26.5 %collective-permute-start.25 = (bf16[512,128]{1,0:T(8,128)(2,1)S(1)}, bf16[512,128]{1,0:T(8,128)(2,1)S(1)}, u32[]{:S(2)}, u32[]{:S(2)}) collective-permute-start(bf16[512,128]{1,0:T(8,128)(2,1)S(1)} %get-tuple-element.63), channel_id=1, source_target_pairs={{0,20},{4,16},{8,28},{12,24},{16,4},{20,0},{24,12},{28,8},{1,21},{... | collective-permute-start | bytes 393224 | tf_op jit(solution)/shard_map/ppermute | solution.py:407
  78.7 24.7 %collective-permute-start.26 = (bf16[512,128]{1,0:T(8,128)(2,1)S(1)}, bf16[512,128]{1,0:T(8,128)(2,1)S(1)}, u32[]{:S(2)}, u32[]{:S(2)}) collective-permute-start(bf16[512,128]{1,0:T(8,128)(2,1)S(1)} %get-tuple-element.64), channel_id=1, source_target_pairs={{0,24},{4,28},{8,16},{12,20},{16,8},{20,12},{24,0},{28,4},{1,25},{... | collective-permute-start | bytes 393224 | tf_op jit(solution)/shard_map/ppermute | solution.py:407
  81.9 23.3 %collective-permute-start.27 = (bf16[512,128]{1,0:T(8,128)(2,1)S(1)}, bf16[512,128]{1,0:T(8,128)(2,1)S(1)}, u32[]{:S(2)}, u32[]{:S(2)}) collective-permute-start(bf16[512,128]{1,0:T(8,128)(2,1)S(1)} %get-tuple-element.65), channel_id=1, source_target_pairs={{0,28},{4,24},{8,20},{12,16},{16,12},{20,8},{24,4},{28,0},{1,29},{... | collective-permute-start | bytes 393224 | tf_op jit(solution)/shard_map/ppermute | solution.py:407
  84.5 24.0 %collective-permute-start.16 = (bf16[512,128]{1,0:T(8,128)(2,1)S(1)}, bf16[512,128]{1,0:T(8,128)(2,1)S(1)}, u32[]{:S(2)}, u32[]{:S(2)}) collective-permute-start(bf16[512,128]{1,0:T(8,128)(2,1)S(1)} %get-tuple-element.54), channel_id=1, source_target_pairs={{0,12},{4,8},{8,4},{12,0},{16,28},{20,24},{24,20},{28,16},{1,13},{... | collective-permute-start | bytes 393224 | tf_op jit(solution)/shard_map/ppermute | solution.py:407
  91.6 24.2 %collective-permute-start.17 = (bf16[512,128]{1,0:T(8,128)(2,1)S(1)}, bf16[512,128]{1,0:T(8,128)(2,1)S(1)}, u32[]{:S(2)}, u32[]{:S(2)}) collective-permute-start(bf16[512,128]{1,0:T(8,128)(2,1)S(1)} %get-tuple-element.55), channel_id=1, source_target_pairs={{0,16},{4,20},{8,24},{12,28},{16,0},{20,4},{24,8},{28,12},{1,17},{... | collective-permute-start | bytes 393224 | tf_op jit(solution)/shard_map/ppermute | solution.py:407
  103.5 15.2 %collective-permute-start.18 = (bf16[512,128]{1,0:T(8,128)(2,1)S(1)}, bf16[512,128]{1,0:T(8,128)(2,1)S(1)}, u32[]{:S(2)}, u32[]{:S(2)}) collective-permute-start(bf16[512,128]{1,0:T(8,128)(2,1)S(1)} %get-tuple-element.56), channel_id=1, source_target_pairs={{0,20},{4,16},{8,28},{12,24},{16,4},{20,0},{24,12},{28,8},{1,21},{... | collective-permute-start | bytes 393224 | tf_op jit(solution)/shard_map/ppermute | solution.py:407
  103.5 15.2 %collective-permute-start.19 = (bf16[512,128]{1,0:T(8,128)(2,1)S(1)}, bf16[512,128]{1,0:T(8,128)(2,1)S(1)}, u32[]{:S(2)}, u32[]{:S(2)}) collective-permute-start(bf16[512,128]{1,0:T(8,128)(2,1)S(1)} %get-tuple-element.57), channel_id=1, source_target_pairs={{0,24},{4,28},{8,16},{12,20},{16,8},{20,12},{24,0},{28,4},{1,25},{... | collective-permute-start | bytes 393224 | tf_op jit(solution)/shard_map/ppermute | solution.py:407
  105.2 13.5 %collective-permute-start.20 = (bf16[512,128]{1,0:T(8,128)(2,1)S(1)}, bf16[512,128]{1,0:T(8,128)(2,1)S(1)}, u32[]{:S(2)}, u32[]{:S(2)}) collective-permute-start(bf16[512,128]{1,0:T(8,128)(2,1)S(1)} %get-tuple-element.58), channel_id=1, source_target_pairs={{0,28},{4,24},{8,20},{12,16},{16,12},{20,8},{24,4},{28,0},{1,29},{... | collective-permute-start | bytes 393224 | tf_op jit(solution)/shard_map/ppermute | solution.py:407
  119.4 4.7 %collective-permute-start.28 = (f32[1,512]{1,0:T(1,128)S(1)}, f32[1,512]{1,0:T(1,128)S(1)}, u32[]{:S(2)}, u32[]{:S(2)}) collective-permute-start(f32[1,512]{1,0:T(1,128)S(1)} %shard_map.76.refs_0_), channel_id=1, source_target_pairs={{0,3},{1,2},{2,1},{3,0},{4,7},{5,6},{6,5},{7,4},{8,11},{9,10},{10,... | collective-permute-start | bytes 6152 | tf_op jit(solution)/shard_map/ppermute | solution.py:461
  119.5 4.6 %collective-permute-start.29 = (f32[1,512]{1,0:T(1,128)S(1)}, f32[1,512]{1,0:T(1,128)S(1)}, u32[]{:S(2)}, u32[]{:S(2)}) collective-permute-start(f32[1,512]{1,0:T(1,128)S(1)} %shard_map.76.refs_0_), channel_id=1, source_target_pairs={{0,2},{1,3},{2,0},{3,1},{4,6},{5,7},{6,4},{7,5},{8,10},{9,11},{10,... | collective-permute-start | bytes 6152 | tf_op jit(solution)/shard_map/ppermute | solution.py:461
  121.1 3.0 %collective-permute-start.30 = (f32[1,512]{1,0:T(1,128)S(1)}, f32[1,512]{1,0:T(1,128)S(1)}, u32[]{:S(2)}, u32[]{:S(2)}) collective-permute-start(f32[1,512]{1,0:T(1,128)S(1)} %shard_map.76.refs_0_), channel_id=1, source_target_pairs={{0,1},{1,0},{2,3},{3,2},{4,5},{5,4},{6,7},{7,6},{8,9},{9,8},{10,11... | collective-permute-start | bytes 6152 | tf_op jit(solution)/shard_map/ppermute | solution.py:461
  122.7 1.4 %copy-start.1 = (f32[2048]{0:T(1024)S(1)}, f32[2048]{0:T(1024)}, u32[]{:S(2)}) copy-start(f32[2048]{0:T(1024)} %param.9) | copy-start | bytes 24580
where the time goes:
time: 127 us; the launch traced here: 126 us
  waiting for transfers between devices  56.8 us (45%)
  starting transfers between devices  44.7 us (35%)
  Pallas kernels  24.1 us (19%)
    ppermute x28, waiting for transfers between devices, exchange(): moved[delta] = lax.ppermute(pieces[delta], 'seq', pairs_of(blocks, delta))  56.8 us
    ppermute x28, starting transfers between devices, exchange(): moved[delta] = lax.ppermute(pieces[delta], 'seq', pairs_of(blocks, delta))  42.7 us
    pallas_call x2, Pallas kernels, make_conv(): pl.pallas_call(functools.partial(conv_kernel, blocks, per_chunk, chunk),...  10.5 us
    pallas_call x3, Pallas kernels, make_product(): pl.pallas_call(functools.partial(product_kernel, blocks, deltas, tokens,...  7.28 us
    pallas_call x2, Pallas kernels, make_gate(): pl.pallas_call(functools.partial(gate_kernel, blocks, chunk, chunks), out...  2.69 us
  transfers between devices with their start and end apart: 31, of which 11 were waited for; matrix products, arithmetic and copies ran while one was open for 0% of the time, Pallas kernels for 11%

commit v1 on v0

--- a/solution.py
+++ b/solution.py
@@ -115,7 +115,7 @@
 LANES = 128
 HALF = 256
 VMEM_BYTES = 20 << 20
-SMALL_BYTES = 10 << 20
+SMALL_BYTES = 14 << 20
 FIRST_BYTES = 62 << 20
 PRODUCT_BYTES = 58 << 20
 ANYWHERE = pl.BlockSpec(memory_space=pl.ANY)
@@ -125,7 +125,7 @@
     (1, 2, 3, 4, 5, 6, 7),
     (1, 2, 3, 4, 5, 6, 7),
 )
-FINISH_ROWS = 256
+FINISH_ROWS = 128
 
 
 def pairs_of(blocks, delta):
@@ -359,42 +359,54 @@
 
 
 def finish_kernel(blocks, chunks, parts, seq_ref, gate_ref, gain_ref, *refs):
-    sums, pieces, normed_ref = refs[:parts], refs[parts:-1], refs[-1]
-    rows = gate_ref.shape[0]
-    square_sum = sums[0][...]
-    for part in sums[1:]:
-        square_sum = square_sum + part[...]
-    inverse = lax.rsqrt(square_sum / D + norm_eps)
-    scale = jnp.transpose(jnp.broadcast_to(inverse, (LANES, rows)))
-    for delta in range(blocks):
-        for chunk in range(chunks):
-            place = pl.multiple_of(((seq_ref[0] ^ delta) * chunks + chunk) * LANES, LANES)
-            columns = pl.ds(place, LANES)
-            piece = pieces[chunk * blocks + delta][...].astype(jnp.float32)
-            gated = gate_ref[:, columns].astype(jnp.float32) * piece
-            normed_ref[:, columns] = (gated * scale * gain_ref[:, columns]).astype(jnp.bfloat16)
+    sums, pieces = refs[:parts], refs[parts:-3]
+    normed_ref, staged, sems = refs[-3:]
+    rows = FINISH_ROWS
+    copies = []
+    for turn in range(gate_ref.shape[0] // rows):
+        lines = pl.ds(turn * rows, rows)
+        square_sum = sums[0][:, lines]
+        for part in sums[1:]:
+            square_sum = square_sum + part[:, lines]
+        inverse = lax.rsqrt(square_sum / D + norm_eps)
+        scale = jnp.transpose(jnp.broadcast_to(inverse, (LANES, rows)))
+        for delta in range(blocks):
+            for chunk in range(chunks):
+                place = pl.multiple_of(((seq_ref[0] ^ delta) * chunks + chunk) * LANES, LANES)
+                columns = pl.ds(place, LANES)
+                piece = pieces[chunk * blocks + delta][lines, :].astype(jnp.float32)
+                gated = gate_ref[lines, columns].astype(jnp.float32) * piece
+                staged[lines, columns] = (gated * scale * gain_ref[:, columns]).astype(jnp.bfloat16)
+        copies.append(
+            pltpu.make_async_copy(staged.at[lines, :], normed_ref.at[lines, :], sems.at[turn])
+        )
+        copies[-1].start()
+    for copy in copies:
+        copy.wait()
 
 
 def make_finish(seq_index, query_gate, norm_gain, sums, pieces, blocks, chunks):
     tokens, channels = query_gate.shape
-    rows = FINISH_ROWS
-    row_spec = pl.BlockSpec((rows, channels), lambda step, seq_ref: (step, 0))
     return pl.pallas_call(
         functools.partial(finish_kernel, blocks, chunks, len(sums)),
         out_shape=jax.ShapeDtypeStruct((tokens, channels), jnp.bfloat16),
         grid_spec=pltpu.PrefetchScalarGridSpec(
             num_scalar_prefetch=1,
-            grid=(tokens // rows,),
+            grid=(1,),
             in_specs=[
-                row_spec,
+                pl.BlockSpec((tokens, channels), lambda step, seq_ref: (0, 0)),
                 pl.BlockSpec((1, channels), lambda step, seq_ref: (0, 0)),
             ]
-            + [pl.BlockSpec((1, rows), lambda step, seq_ref: (0, step))] * len(sums)
-            + [pl.BlockSpec((rows, LANES), lambda step, seq_ref: (step, 0))] * (blocks * chunks),
-            out_specs=row_spec,
+            + [pl.BlockSpec((1, tokens), lambda step, seq_ref: (0, 0))] * len(sums)
+            + [pl.BlockSpec((tokens, LANES), lambda step, seq_ref: (0, 0))] * (blocks * chunks),
+            out_specs=ANYWHERE,
+            scratch_shapes=[
+                pltpu.VMEM((tokens, channels), jnp.bfloat16),
+                pltpu.SemaphoreType.DMA((tokens // FINISH_ROWS,)),
+            ],
         ),
         cost_estimate=pl.CostEstimate(
-            flops=4 * tokens * channels, bytes_accessed=8 * tokens * channels, transcendentals=tokens
+            flops=4 * tokens * channels, bytes_accessed=6 * tokens * channels, transcendentals=tokens
         ),
         compiler_params=pltpu.CompilerParams(vmem_limit_bytes=SMALL_BYTES),
         name="finish",

time: 127 us -> 127 us (level)
  no operation moved by 1% of the time
where the time goes in v1:
time: 127 us; the launch traced here: 126 us
  waiting for transfers between devices  56.8 us (45%)
  starting transfers between devices  44.7 us (35%)
  Pallas kernels  23.7 us (19%)
    ppermute x28, waiting for transfers between devices, exchange(): moved[delta] = lax.ppermute(pieces[delta], 'seq', pairs_of(blocks, delta))  56.8 us
    ppermute x28, starting transfers between devices, exchange(): moved[delta] = lax.ppermute(pieces[delta], 'seq', pairs_of(blocks, delta))  42.7 us
    pallas_call x2, Pallas kernels, make_conv(): pl.pallas_call(functools.partial(conv_kernel, blocks, per_chunk, chunk),...  10.5 us
    pallas_call x3, Pallas kernels, make_product(): pl.pallas_call(functools.partial(product_kernel, blocks, deltas, tokens,...  7.28 us
    pallas_call x2, Pallas kernels, make_gate(): pl.pallas_call(functools.partial(gate_kernel, blocks, chunk, chunks), out...  2.69 us
  transfers between devices with their start and end apart: 31, of which 11 were waited for; matrix products, arithmetic and copies ran while one was open for 0% of the time, Pallas kernels for 11%

profile of v1, /device:TPU:0, one launch (start us, length us, event | category | flops | bytes accessed | tf_op | source)
XLA Modules:
  0.0 126.2 jit_solution(945978087810497161)
XLA Ops:
  0.6 2.3 %shard_map.69 = (bf16[528,128]{1,0:T(8,128)(2,1)}, bf16[528,128]{1,0:T(8,128)(2,1)}, bf16[528,128]{1,0:T(8,128)(2,1)}, bf16[528,128]{1,0:T(8,128)(2,1)}) custom-call(s32[1]{0:T(128)} %bitcast.seq_ref, bf16[512,2048]{1,0:T(8,128)(2,1)} %refs_3_.9, bf16[512,2048]{1,0:T(8,128)(2,1)} %refs_3_.9, bf16[512,2048]{1,0:T(8,128)(2,1)} %refs_3_.9, ...), custom_call_target="tpu_custom_call" | custom-call | flops 262144 | bytes 1572864 | tf_op jit(solution)/shard_map/pallas_call | solution.py:174
  2.9 3.0 %collective-permute-start.7 = (bf16[528,128]{1,0:T(8,128)(2,1)}, bf16[528,128]{1,0:T(8,128)(2,1)S(1)}, u32[]{:S(2)}, u32[]{:S(2)}) collective-permute-start(bf16[528,128]{1,0:T(8,128)(2,1)} %get-tuple-element.43), channel_id=1, source_target_pairs={{0,4},{4,0},{8,12},{12,8},{16,20},{20,16},{24,28},{28,24},{1,5},{5... | collective-permute-start | bytes 405512 | tf_op jit(solution)/shard_map/ppermute | solution.py:419
  5.9 1.6 %collective-permute-start.8 = (bf16[528,128]{1,0:T(8,128)(2,1)}, bf16[528,128]{1,0:T(8,128)(2,1)S(1)}, u32[]{:S(2)}, u32[]{:S(2)}) collective-permute-start(bf16[528,128]{1,0:T(8,128)(2,1)} %get-tuple-element.44), channel_id=1, source_target_pairs={{0,8},{4,12},{8,0},{12,4},{16,24},{20,28},{24,16},{28,20},{1,9},{5... | collective-permute-start | bytes 405512 | tf_op jit(solution)/shard_map/ppermute | solution.py:419
  7.5 2.7 %shard_map.68 = (bf16[512,128]{1,0:T(8,128)(2,1)}, bf16[512,128]{1,0:T(8,128)(2,1)}, bf16[512,128]{1,0:T(8,128)(2,1)}, bf16[512,128]{1,0:T(8,128)(2,1)}, bf16[51...) custom-call(s32[1]{0:T(128)} %bitcast.seq_ref, ...), custom_call_target="tpu_custom_call" | custom-call | flops 524288 | bytes 3145728 | tf_op jit(solution)/shard_map/pallas_call | solution.py:174
  10.2 0.5 collective-permute-start
  10.7 0.0 collective-permute-start.1
  10.8 0.0 copy-start.2
  10.8 3.0 %collective-permute-start.9 = (bf16[528,128]{1,0:T(8,128)(2,1)S(1)}, bf16[528,128]{1,0:T(8,128)(2,1)S(1)}, u32[]{:S(2)}, u32[]{:S(2)}) collective-permute-start(bf16[528,128]{1,0:T(8,128)(2,1)S(1)} %copy-done.4), channel_id=1, source_target_pairs={{0,12},{4,8},{8,4},{12,0},{16,28},{20,24},{24,20},{28,16},{1,13},{... | collective-permute-start | bytes 405512 | tf_op jit(solution)/shard_map/ppermute | solution.py:419
  13.8 2.3 %shard_map.70 = (bf16[528,128]{1,0:T(8,128)(2,1)}, bf16[528,128]{1,0:T(8,128)(2,1)}, bf16[528,128]{1,0:T(8,128)(2,1)}, bf16[528,128]{1,0:T(8,128)(2,1)}) custom-call(s32[1]{0:T(128)} %bitcast.seq_ref, bf16[512,2048]{1,0:T(8,128)(2,1)} %refs_3_.9, bf16[512,2048]{1,0:T(8,128)(2,1)} %refs_3_.9, bf16[512,2048]{1,0:T(8,128)(2,1)} %refs_3_.9, ...), custom_call_target="tpu_custom_call" | custom-call | flops 262144 | bytes 1572864 | tf_op jit(solution)/shard_map/pallas_call | solution.py:174
  16.1 0.4 collective-permute-done.refs_1_
  16.4 2.6 %collective-permute-start.10 = (bf16[528,128]{1,0:T(8,128)(2,1)}, bf16[528,128]{1,0:T(8,128)(2,1)S(1)}, u32[]{:S(2)}, u32[]{:S(2)}) collective-permute-start(bf16[528,128]{1,0:T(8,128)(2,1)} %get-tuple-element.46), channel_id=1, source_target_pairs={{0,16},{4,20},{8,24},{12,28},{16,0},{20,4},{24,8},{28,12},{1,17},{... | collective-permute-start | bytes 405512 | tf_op jit(solution)/shard_map/ppermute | solution.py:419
  19.0 1.8 %collective-permute-start.11 = (bf16[528,128]{1,0:T(8,128)(2,1)}, bf16[528,128]{1,0:T(8,128)(2,1)S(1)}, u32[]{:S(2)}, u32[]{:S(2)}) collective-permute-start(bf16[528,128]{1,0:T(8,128)(2,1)} %get-tuple-element.47), channel_id=1, source_target_pairs={{0,20},{4,16},{8,28},{12,24},{16,4},{20,0},{24,12},{28,8},{1,21},{... | collective-permute-start | bytes 405512 | tf_op jit(solution)/shard_map/ppermute | solution.py:419
  20.8 0.7 collective-permute-start.12
  21.5 3.1 %collective-permute-start.13 = (bf16[528,128]{1,0:T(8,128)(2,1)}, bf16[528,128]{1,0:T(8,128)(2,1)S(1)}, u32[]{:S(2)}, u32[]{:S(2)}) collective-permute-start(bf16[528,128]{1,0:T(8,128)(2,1)} %get-tuple-element.49), channel_id=1, source_target_pairs={{0,28},{4,24},{8,20},{12,16},{16,12},{20,8},{24,4},{28,0},{1,29},{... | collective-permute-start | bytes 405512 | tf_op jit(solution)/shard_map/ppermute | solution.py:419
  24.6 10.7 %collective-permute-done.10.refs_4_.refs_12_ = bf16[528,128]{1,0:T(8,128)(2,1)S(1)} collective-permute-done((bf16[528,128]{1,0:T(8,128)(2,1)}, bf16[528,128]{1,0:T(8,128)(2,1)S(1)}, u32[]{:S(2)}, u32[]{:S(2)}) %collective-permute-start.10) | collective-permute-done | bytes 135200 | tf_op jit(solution)/shard_map/ppermute | solution.py:419
  35.3 3.5 %collective-permute-done.11.refs_5_.refs_13_ = bf16[528,128]{1,0:T(8,128)(2,1)S(1)} collective-permute-done((bf16[528,128]{1,0:T(8,128)(2,1)}, bf16[528,128]{1,0:T(8,128)(2,1)S(1)}, u32[]{:S(2)}, u32[]{:S(2)}) %collective-permute-start.11) | collective-permute-done | bytes 135200 | tf_op jit(solution)/shard_map/ppermute | solution.py:419
  38.8 1.9 %collective-permute-start.5 = (bf16[512,128]{1,0:T(8,128)(2,1)S(1)}, bf16[512,128]{1,0:T(8,128)(2,1)S(1)}, u32[]{:S(2)}, u32[]{:S(2)}) collective-permute-start(bf16[512,128]{1,0:T(8,128)(2,1)S(1)} %copy-done.6), channel_id=1, source_target_pairs={{0,24},{4,28},{8,16},{12,20},{16,8},{20,12},{24,0},{28,4},{1,25},{... | collective-permute-start | bytes 393224 | tf_op jit(solution)/shard_map/ppermute | solution.py:419
  40.7 2.6 %collective-permute-start.6 = (bf16[512,128]{1,0:T(8,128)(2,1)S(1)}, bf16[512,128]{1,0:T(8,128)(2,1)S(1)}, u32[]{:S(2)}, u32[]{:S(2)}) collective-permute-start(bf16[512,128]{1,0:T(8,128)(2,1)S(1)} %copy-done.5), channel_id=1, source_target_pairs={{0,28},{4,24},{8,20},{12,16},{16,12},{20,8},{24,4},{28,0},{1,29},{... | collective-permute-start | bytes 393224 | tf_op jit(solution)/shard_map/ppermute | solution.py:419
  43.3 5.3 %shard_map.71 = (bf16[512,128]{1,0:T(8,128)(2,1)S(1)}, bf16[512,128]{1,0:T(8,128)(2,1)S(1)}, bf16[512,128]{1,0:T(8,128)(2,1)S(1)}, bf16[512,128]{1,0:T(8,128)(2,...) custom-call(s32[1]{0:T(128)} %bitcast.seq_ref, ...), custom_call_target="tpu_custom_call" | custom-call | flops 9663676416 | bytes 2097152 | tf_op jit(solution)/shard_map/pallas_call | solution.py:258
  48.6 8.3 %collective-permute-done.3.refs_4_ = bf16[512,128]{1,0:T(8,128)(2,1)S(1)} collective-permute-done((bf16[512,128]{1,0:T(8,128)(2,1)S(1)}, bf16[512,128]{1,0:T(8,128)(2,1)S(1)}, u32[]{:S(2)}, u32[]{:S(2)}) %collective-permute-start.3) | collective-permute-done | bytes 131104 | tf_op jit(solution)/shard_map/ppermute | solution.py:419
  57.0 3.1 %collective-permute-done.4.refs_5_ = bf16[512,128]{1,0:T(8,128)(2,1)S(1)} collective-permute-done((bf16[512,128]{1,0:T(8,128)(2,1)S(1)}, bf16[512,128]{1,0:T(8,128)(2,1)S(1)}, u32[]{:S(2)}, u32[]{:S(2)}) %collective-permute-start.4) | collective-permute-done | bytes 131104 | tf_op jit(solution)/shard_map/ppermute | solution.py:419
  60.0 0.0 copy-start
  60.1 5.3 %shard_map.72 = (bf16[512,128]{1,0:T(8,128)(2,1)S(1)}, bf16[512,128]{1,0:T(8,128)(2,1)S(1)}, bf16[512,128]{1,0:T(8,128)(2,1)S(1)}, bf16[512,128]{1,0:T(8,128)(2,...) custom-call(s32[1]{0:T(128)} %bitcast.seq_ref, ...), custom_call_target="tpu_custom_call" | custom-call | flops 9663676416 | bytes 2097152 | tf_op jit(solution)/shard_map/pallas_call | solution.py:258
  65.3 1.3 collective-permute-start.14
  66.6 4.7 %collective-permute-start.15 = (bf16[512,128]{1,0:T(8,128)(2,1)S(1)}, bf16[512,128]{1,0:T(8,128)(2,1)S(1)}, u32[]{:S(2)}, u32[]{:S(2)}) collective-permute-start(bf16[512,128]{1,0:T(8,128)(2,1)S(1)} %get-tuple-element.53), channel_id=1, source_target_pairs={{0,8},{4,12},{8,0},{12,4},{16,24},{20,28},{24,16},{28,20},{1,9},{5... | collective-permute-start | bytes 393224 | tf_op jit(solution)/shard_map/ppermute | solution.py:419
  71.3 1.0 collective-permute-start.21
  72.3 2.5 %collective-permute-start.23 = (bf16[512,128]{1,0:T(8,128)(2,1)S(1)}, bf16[512,128]{1,0:T(8,128)(2,1)S(1)}, u32[]{:S(2)}, u32[]{:S(2)}) collective-permute-start(bf16[512,128]{1,0:T(8,128)(2,1)S(1)} %get-tuple-element.61), channel_id=1, source_target_pairs={{0,12},{4,8},{8,4},{12,0},{16,28},{20,24},{24,20},{28,16},{1,13},{... | collective-permute-start | bytes 393224 | tf_op jit(solution)/shard_map/ppermute | solution.py:419
  74.8 2.0 %collective-permute-start.24 = (bf16[512,128]{1,0:T(8,128)(2,1)S(1)}, bf16[512,128]{1,0:T(8,128)(2,1)S(1)}, u32[]{:S(2)}, u32[]{:S(2)}) collective-permute-start(bf16[512,128]{1,0:T(8,128)(2,1)S(1)} %get-tuple-element.62), channel_id=1, source_target_pairs={{0,16},{4,20},{8,24},{12,28},{16,0},{20,4},{24,8},{28,12},{1,17},{... | collective-permute-start | bytes 393224 | tf_op jit(solution)/shard_map/ppermute | solution.py:419
  76.8 0.2 collective-permute-done.15.refs_10_.refs_14_
  77.0 1.7 %collective-permute-start.25 = (bf16[512,128]{1,0:T(8,128)(2,1)S(1)}, bf16[512,128]{1,0:T(8,128)(2,1)S(1)}, u32[]{:S(2)}, u32[]{:S(2)}) collective-permute-start(bf16[512,128]{1,0:T(8,128)(2,1)S(1)} %get-tuple-element.63), channel_id=1, source_target_pairs={{0,20},{4,16},{8,28},{12,24},{16,4},{20,0},{24,12},{28,8},{1,21},{... | collective-permute-start | bytes 393224 | tf_op jit(solution)/shard_map/ppermute | solution.py:419
  78.7 1.7 %collective-permute-start.26 = (bf16[512,128]{1,0:T(8,128)(2,1)S(1)}, bf16[512,128]{1,0:T(8,128)(2,1)S(1)}, u32[]{:S(2)}, u32[]{:S(2)}) collective-permute-start(bf16[512,128]{1,0:T(8,128)(2,1)S(1)} %get-tuple-element.64), channel_id=1, source_target_pairs={{0,24},{4,28},{8,16},{12,20},{16,8},{20,12},{24,0},{28,4},{1,25},{... | collective-permute-start | bytes 393224 | tf_op jit(solution)/shard_map/ppermute | solution.py:419
  80.5 1.4 %collective-permute-done.22.refs_10_.refs_6_ = bf16[512,128]{1,0:T(8,128)(2,1)S(1)} collective-permute-done((bf16[512,128]{1,0:T(8,128)(2,1)S(1)}, bf16[512,128]{1,0:T(8,128)(2,1)S(1)}, u32[]{:S(2)}, u32[]{:S(2)}) %collective-permute-start.22) | collective-permute-done | bytes 131104 | tf_op jit(solution)/shard_map/ppermute | solution.py:419
  81.9 2.6 %collective-permute-start.27 = (bf16[512,128]{1,0:T(8,128)(2,1)S(1)}, bf16[512,128]{1,0:T(8,128)(2,1)S(1)}, u32[]{:S(2)}, u32[]{:S(2)}) collective-permute-start(bf16[512,128]{1,0:T(8,128)(2,1)S(1)} %get-tuple-element.65), channel_id=1, source_target_pairs={{0,28},{4,24},{8,20},{12,16},{16,12},{20,8},{24,4},{28,0},{1,29},{... | collective-permute-start | bytes 393224 | tf_op jit(solution)/shard_map/ppermute | solution.py:419
  84.5 7.1 %collective-permute-done.24.refs_12_.refs_8_ = bf16[512,128]{1,0:T(8,128)(2,1)S(1)} collective-permute-done((bf16[512,128]{1,0:T(8,128)(2,1)S(1)}, bf16[512,128]{1,0:T(8,128)(2,1)S(1)}, u32[]{:S(2)}, u32[]{:S(2)}) %collective-permute-start.24) | collective-permute-done | bytes 131104 | tf_op jit(solution)/shard_map/ppermute | solution.py:419
  91.6 11.9 %collective-permute-done.25.refs_13_.refs_9_ = bf16[512,128]{1,0:T(8,128)(2,1)S(1)} collective-permute-done((bf16[512,128]{1,0:T(8,128)(2,1)S(1)}, bf16[512,128]{1,0:T(8,128)(2,1)S(1)}, u32[]{:S(2)}, u32[]{:S(2)}) %collective-permute-start.25) | collective-permute-done | bytes 131104 | tf_op jit(solution)/shard_map/ppermute | solution.py:419
  103.5 1.7 %collective-permute-start.19 = (bf16[512,128]{1,0:T(8,128)(2,1)S(1)}, bf16[512,128]{1,0:T(8,128)(2,1)S(1)}, u32[]{:S(2)}, u32[]{:S(2)}) collective-permute-start(bf16[512,128]{1,0:T(8,128)(2,1)S(1)} %get-tuple-element.57), channel_id=1, source_target_pairs={{0,24},{4,28},{8,16},{12,20},{16,8},{20,12},{24,0},{28,4},{1,25},{... | collective-permute-start | bytes 393224 | tf_op jit(solution)/shard_map/ppermute | solution.py:419
  105.2 2.7 %collective-permute-start.20 = (bf16[512,128]{1,0:T(8,128)(2,1)S(1)}, bf16[512,128]{1,0:T(8,128)(2,1)S(1)}, u32[]{:S(2)}, u32[]{:S(2)}) collective-permute-start(bf16[512,128]{1,0:T(8,128)(2,1)S(1)} %get-tuple-element.58), channel_id=1, source_target_pairs={{0,28},{4,24},{8,20},{12,16},{16,12},{20,8},{24,4},{28,0},{1,29},{... | collective-permute-start | bytes 393224 | tf_op jit(solution)/shard_map/ppermute | solution.py:419
  107.9 0.5 shard_map.75.refs_16_
  108.5 7.3 %collective-permute-done.17.refs_12_.refs_16_ = bf16[512,128]{1,0:T(8,128)(2,1)S(1)} collective-permute-done((bf16[512,128]{1,0:T(8,128)(2,1)S(1)}, bf16[512,128]{1,0:T(8,128)(2,1)S(1)}, u32[]{:S(2)}, u32[]{:S(2)}) %collective-permute-start.17) | collective-permute-done | bytes 131104 | tf_op jit(solution)/shard_map/ppermute | solution.py:419
  115.8 2.9 %collective-permute-done.18.refs_13_.refs_17_ = bf16[512,128]{1,0:T(8,128)(2,1)S(1)} collective-permute-done((bf16[512,128]{1,0:T(8,128)(2,1)S(1)}, bf16[512,128]{1,0:T(8,128)(2,1)S(1)}, u32[]{:S(2)}, u32[]{:S(2)}) %collective-permute-start.18) | collective-permute-done | bytes 131104 | tf_op jit(solution)/shard_map/ppermute | solution.py:419
  118.7 0.7 shard_map.76.refs_0_
  119.4 0.1 collective-permute-start.28
  119.5 1.6 %collective-permute-start.29 = (f32[1,512]{1,0:T(1,128)S(1)}, f32[1,512]{1,0:T(1,128)S(1)}, u32[]{:S(2)}, u32[]{:S(2)}) collective-permute-start(f32[1,512]{1,0:T(1,128)S(1)} %shard_map.76.refs_0_), channel_id=1, source_target_pairs={{0,2},{1,3},{2,0},{3,1},{4,6},{5,7},{6,4},{7,5},{8,10},{9,11},{10,... | collective-permute-start | bytes 6152 | tf_op jit(solution)/shard_map/ppermute | solution.py:473
  121.1 0.3 collective-permute-start.30
  121.3 1.3 %shard_map.73.refs_16_ = bf16[512,2048]{1,0:T(8,128)(2,1)} custom-call(s32[1]{0:T(128)} %bitcast.seq_ref, bf16[512,2048]{1,0:T(8,128)(2,1)S(1)} %copy-done, bf16[512,2048]{1,0:T(8,128)(2,1)S(1)} %copy-done, bf16[512,2048]{1,0:T(8,128)(2,1)S(1)} %copy-done, bf16[512,2048]{1,0:T(8,128)(2,1)S(1)} %copy-done, bf16[512,2048]{1,0:T(8,128)(2,1)S(1)} %copy-done, ...), custom_call_target="tpu_custom_call" | custom-call | flops 524288 | bytes 3145728 | tf_op jit(solution)/shard_map/pallas_call | solution.py:335
  122.7 0.0 copy-start.1
  122.7 1.4 %shard_map.74 = bf16[512,2048]{1,0:T(8,128)(2,1)} custom-call(s32[1]{0:T(128)} %bitcast.seq_ref, bf16[512,2048]{1,0:T(8,128)(2,1)S(1)} %copy-done, bf16[512,2048]{1,0:T(8,128)(2,1)S(1)} %copy-done, bf16[512,2048]{1,0:T(8,128)(2,1)S(1)} %copy-done, bf16[512,2048]{1,0:T(8,128)(2,1)S(1)} %copy-done, ...), custom_call_target="tpu_custom_call", output_to_operand_aliasing={{}: (17, {})} | custom-call | flops 524288 | bytes 3145728 | tf_op jit(solution)/shard_map/pallas_call | solution.py:335
  124.1 1.9 %finish.1 = bf16[512,2048]{1,0:T(8,128)(2,1)} custom-call(s32[1]{0:T(128)} %bitcast.seq_ref, bf16[512,2048]{1,0:T(8,128)(2,1)S(1)} %copy-done, f32[1,2048]{1,0:T(1,128)S(1)} %bitcast.3, f32[1,512]{1,0:T(1,128)S(1)} %shard_map.76.refs_0_, f32[1,512]{1,0:T(1,128)S(1)} %collective-permute-done.28.refs_1_, f32[1,512]{1,0:T(1,128)S(1)} %collective-permute-done.29.refs_2_, ...), custom_call_target="tpu_custom_call" | custom-call | flops 4194304 | bytes 6291456 | tf_op jit(solution)/shard_map/finish/pallas_call | solution.py:390
  (44 shorter events, 0.1 us)
Async XLA Ops:
  2.9 17.9 %collective-permute-start.7 = (bf16[528,128]{1,0:T(8,128)(2,1)}, bf16[528,128]{1,0:T(8,128)(2,1)S(1)}, u32[]{:S(2)}, u32[]{:S(2)}) collective-permute-start(bf16[528,128]{1,0:T(8,128)(2,1)} %get-tuple-element.43), channel_id=1, source_target_pairs={{0,4},{4,0},{8,12},{12,8},{16,20},{20,16},{24,28},{28,24},{1,5},{5... | collective-permute-start | bytes 405512 | tf_op jit(solution)/shard_map/ppermute | solution.py:419
  5.9 4.9 %copy-start.4 = (bf16[528,128]{1,0:T(8,128)(2,1)S(1)}, bf16[528,128]{1,0:T(8,128)(2,1)}, u32[]{:S(2)}) copy-start(bf16[528,128]{1,0:T(8,128)(2,1)} %get-tuple-element.45) | copy-start | bytes 405508
  5.9 15.6 %collective-permute-start.8 = (bf16[528,128]{1,0:T(8,128)(2,1)}, bf16[528,128]{1,0:T(8,128)(2,1)S(1)}, u32[]{:S(2)}, u32[]{:S(2)}) collective-permute-start(bf16[528,128]{1,0:T(8,128)(2,1)} %get-tuple-element.44), channel_id=1, source_target_pairs={{0,8},{4,12},{8,0},{12,4},{16,24},{20,28},{24,16},{28,20},{1,9},{5... | collective-permute-start | bytes 405512 | tf_op jit(solution)/shard_map/ppermute | solution.py:419
  10.2 6.3 %collective-permute-start = (bf16[512,128]{1,0:T(8,128)(2,1)}, bf16[512,128]{1,0:T(8,128)(2,1)S(1)}, u32[]{:S(2)}, u32[]{:S(2)}) collective-permute-start(bf16[512,128]{1,0:T(8,128)(2,1)} %get-tuple-element.35), channel_id=1, source_target_pairs={{0,4},{4,0},{8,12},{12,8},{16,20},{20,16},{24,28},{28,24},{1,5},{5... | collective-permute-start | bytes 393224 | tf_op jit(solution)/shard_map/ppermute | solution.py:419
  10.7 8.3 %collective-permute-start.1 = (bf16[512,128]{1,0:T(8,128)(2,1)}, bf16[512,128]{1,0:T(8,128)(2,1)S(1)}, u32[]{:S(2)}, u32[]{:S(2)}) collective-permute-start(bf16[512,128]{1,0:T(8,128)(2,1)} %get-tuple-element.36), channel_id=1, source_target_pairs={{0,8},{4,12},{8,0},{12,4},{16,24},{20,28},{24,16},{28,20},{1,9},{5... | collective-permute-start | bytes 393224 | tf_op jit(solution)/shard_map/ppermute | solution.py:419
  10.8 13.9 %copy-start.9 = (bf16[512,128]{1,0:T(8,128)(2,1)S(1)}, bf16[512,128]{1,0:T(8,128)(2,1)}, u32[]{:S(2)}) copy-start(bf16[512,128]{1,0:T(8,128)(2,1)} %get-tuple-element.37) | copy-start | bytes 393220
  10.8 24.5 %copy-start.8 = (bf16[512,128]{1,0:T(8,128)(2,1)S(1)}, bf16[512,128]{1,0:T(8,128)(2,1)}, u32[]{:S(2)}) copy-start(bf16[512,128]{1,0:T(8,128)(2,1)} %get-tuple-element.38) | copy-start | bytes 393220
  10.8 28.0 %copy-start.7 = (bf16[512,128]{1,0:T(8,128)(2,1)S(1)}, bf16[512,128]{1,0:T(8,128)(2,1)}, u32[]{:S(2)}) copy-start(bf16[512,128]{1,0:T(8,128)(2,1)} %get-tuple-element.39) | copy-start | bytes 393220
  10.8 28.0 %copy-start.6 = (bf16[512,128]{1,0:T(8,128)(2,1)S(1)}, bf16[512,128]{1,0:T(8,128)(2,1)}, u32[]{:S(2)}) copy-start(bf16[512,128]{1,0:T(8,128)(2,1)} %get-tuple-element.40) | copy-start | bytes 393220
  10.8 30.0 %copy-start.5 = (bf16[512,128]{1,0:T(8,128)(2,1)S(1)}, bf16[512,128]{1,0:T(8,128)(2,1)}, u32[]{:S(2)}) copy-start(bf16[512,128]{1,0:T(8,128)(2,1)} %get-tuple-element.41) | copy-start | bytes 393220
  10.8 32.6 %copy-start.2 = (bf16[528,128]{1,0:T(8,128)(2,1)S(1)}, bf16[528,128]{1,0:T(8,128)(2,1)}, u32[]{:S(2)}) copy-start(bf16[528,128]{1,0:T(8,128)(2,1)} %get-tuple-element.42.refs_0_.refs_8_) | copy-start | bytes 405508
  10.8 13.8 %collective-permute-start.9 = (bf16[528,128]{1,0:T(8,128)(2,1)S(1)}, bf16[528,128]{1,0:T(8,128)(2,1)S(1)}, u32[]{:S(2)}, u32[]{:S(2)}) collective-permute-start(bf16[528,128]{1,0:T(8,128)(2,1)S(1)} %copy-done.4), channel_id=1, source_target_pairs={{0,12},{4,8},{8,4},{12,0},{16,28},{20,24},{24,20},{28,16},{1,13},{... | collective-permute-start | bytes 405512 | tf_op jit(solution)/shard_map/ppermute | solution.py:419
  16.4 18.9 %collective-permute-start.10 = (bf16[528,128]{1,0:T(8,128)(2,1)}, bf16[528,128]{1,0:T(8,128)(2,1)S(1)}, u32[]{:S(2)}, u32[]{:S(2)}) collective-permute-start(bf16[528,128]{1,0:T(8,128)(2,1)} %get-tuple-element.46), channel_id=1, source_target_pairs={{0,16},{4,20},{8,24},{12,28},{16,0},{20,4},{24,8},{28,12},{1,17},{... | collective-permute-start | bytes 405512 | tf_op jit(solution)/shard_map/ppermute | solution.py:419
  19.0 19.7 %collective-permute-start.11 = (bf16[528,128]{1,0:T(8,128)(2,1)}, bf16[528,128]{1,0:T(8,128)(2,1)S(1)}, u32[]{:S(2)}, u32[]{:S(2)}) collective-permute-start(bf16[528,128]{1,0:T(8,128)(2,1)} %get-tuple-element.47), channel_id=1, source_target_pairs={{0,20},{4,16},{8,28},{12,24},{16,4},{20,0},{24,12},{28,8},{1,21},{... | collective-permute-start | bytes 405512 | tf_op jit(solution)/shard_map/ppermute | solution.py:419
  20.8 18.0 %collective-permute-start.12 = (bf16[528,128]{1,0:T(8,128)(2,1)}, bf16[528,128]{1,0:T(8,128)(2,1)S(1)}, u32[]{:S(2)}, u32[]{:S(2)}) collective-permute-start(bf16[528,128]{1,0:T(8,128)(2,1)} %get-tuple-element.48), channel_id=1, source_target_pairs={{0,24},{4,28},{8,16},{12,20},{16,8},{20,12},{24,0},{28,4},{1,25},{... | collective-permute-start | bytes 405512 | tf_op jit(solution)/shard_map/ppermute | solution.py:419
  21.5 19.2 %collective-permute-start.13 = (bf16[528,128]{1,0:T(8,128)(2,1)}, bf16[528,128]{1,0:T(8,128)(2,1)S(1)}, u32[]{:S(2)}, u32[]{:S(2)}) collective-permute-start(bf16[528,128]{1,0:T(8,128)(2,1)} %get-tuple-element.49), channel_id=1, source_target_pairs={{0,28},{4,24},{8,20},{12,16},{16,12},{20,8},{24,4},{28,0},{1,29},{... | collective-permute-start | bytes 405512 | tf_op jit(solution)/shard_map/ppermute | solution.py:419
  24.6 24.0 %collective-permute-start.2 = (bf16[512,128]{1,0:T(8,128)(2,1)S(1)}, bf16[512,128]{1,0:T(8,128)(2,1)S(1)}, u32[]{:S(2)}, u32[]{:S(2)}) collective-permute-start(bf16[512,128]{1,0:T(8,128)(2,1)S(1)} %copy-done.9), channel_id=1, source_target_pairs={{0,12},{4,8},{8,4},{12,0},{16,28},{20,24},{24,20},{28,16},{1,13},{... | collective-permute-start | bytes 393224 | tf_op jit(solution)/shard_map/ppermute | solution.py:419
  35.3 21.6 %collective-permute-start.3 = (bf16[512,128]{1,0:T(8,128)(2,1)S(1)}, bf16[512,128]{1,0:T(8,128)(2,1)S(1)}, u32[]{:S(2)}, u32[]{:S(2)}) collective-permute-start(bf16[512,128]{1,0:T(8,128)(2,1)S(1)} %copy-done.8), channel_id=1, source_target_pairs={{0,16},{4,20},{8,24},{12,28},{16,0},{20,4},{24,8},{28,12},{1,17},{... | collective-permute-start | bytes 393224 | tf_op jit(solution)/shard_map/ppermute | solution.py:419
  38.8 21.2 %collective-permute-start.4 = (bf16[512,128]{1,0:T(8,128)(2,1)S(1)}, bf16[512,128]{1,0:T(8,128)(2,1)S(1)}, u32[]{:S(2)}, u32[]{:S(2)}) collective-permute-start(bf16[512,128]{1,0:T(8,128)(2,1)S(1)} %copy-done.7), channel_id=1, source_target_pairs={{0,20},{4,16},{8,28},{12,24},{16,4},{20,0},{24,12},{28,8},{1,21},{... | collective-permute-start | bytes 393224 | tf_op jit(solution)/shard_map/ppermute | solution.py:419
  38.8 21.2 %collective-permute-start.5 = (bf16[512,128]{1,0:T(8,128)(2,1)S(1)}, bf16[512,128]{1,0:T(8,128)(2,1)S(1)}, u32[]{:S(2)}, u32[]{:S(2)}) collective-permute-start(bf16[512,128]{1,0:T(8,128)(2,1)S(1)} %copy-done.6), channel_id=1, source_target_pairs={{0,24},{4,28},{8,16},{12,20},{16,8},{20,12},{24,0},{28,4},{1,25},{... | collective-permute-start | bytes 393224 | tf_op jit(solution)/shard_map/ppermute | solution.py:419
  40.7 19.3 %collective-permute-start.6 = (bf16[512,128]{1,0:T(8,128)(2,1)S(1)}, bf16[512,128]{1,0:T(8,128)(2,1)S(1)}, u32[]{:S(2)}, u32[]{:S(2)}) collective-permute-start(bf16[512,128]{1,0:T(8,128)(2,1)S(1)} %copy-done.5), channel_id=1, source_target_pairs={{0,28},{4,24},{8,20},{12,16},{16,12},{20,8},{24,4},{28,0},{1,29},{... | collective-permute-start | bytes 393224 | tf_op jit(solution)/shard_map/ppermute | solution.py:419
  43.3 16.7 %copy-start.3 = (bf16[512,128]{1,0:T(8,128)(2,1)S(1)}, bf16[512,128]{1,0:T(8,128)(2,1)}, u32[]{:S(2)}) copy-start(bf16[512,128]{1,0:T(8,128)(2,1)} %get-tuple-element.34.refs_0_) | copy-start | bytes 393220
  60.0 47.9 %copy-start = (bf16[512,2048]{1,0:T(8,128)(2,1)S(1)}, bf16[512,2048]{1,0:T(8,128)(2,1)}, u32[]{:S(2)}) copy-start(bf16[512,2048]{1,0:T(8,128)(2,1)} %gate_ref.1) | copy-start | bytes 6291460
  65.3 9.5 %collective-permute-start.14 = (bf16[512,128]{1,0:T(8,128)(2,1)S(1)}, bf16[512,128]{1,0:T(8,128)(2,1)S(1)}, u32[]{:S(2)}, u32[]{:S(2)}) collective-permute-start(bf16[512,128]{1,0:T(8,128)(2,1)S(1)} %get-tuple-element.52), channel_id=1, source_target_pairs={{0,4},{4,0},{8,12},{12,8},{16,20},{20,16},{24,28},{28,24},{1,5},{5... | collective-permute-start | bytes 393224 | tf_op jit(solution)/shard_map/ppermute | solution.py:419
  66.6 10.4 %collective-permute-start.15 = (bf16[512,128]{1,0:T(8,128)(2,1)S(1)}, bf16[512,128]{1,0:T(8,128)(2,1)S(1)}, u32[]{:S(2)}, u32[]{:S(2)}) collective-permute-start(bf16[512,128]{1,0:T(8,128)(2,1)S(1)} %get-tuple-element.53), channel_id=1, source_target_pairs={{0,8},{4,12},{8,0},{12,4},{16,24},{20,28},{24,16},{28,20},{1,9},{5... | collective-permute-start | bytes 393224 | tf_op jit(solution)/shard_map/ppermute | solution.py:419
  71.3 7.4 %collective-permute-start.21 = (bf16[512,128]{1,0:T(8,128)(2,1)S(1)}, bf16[512,128]{1,0:T(8,128)(2,1)S(1)}, u32[]{:S(2)}, u32[]{:S(2)}) collective-permute-start(bf16[512,128]{1,0:T(8,128)(2,1)S(1)} %get-tuple-element.59), channel_id=1, source_target_pairs={{0,4},{4,0},{8,12},{12,8},{16,20},{20,16},{24,28},{28,24},{1,5},{5... | collective-permute-start | bytes 393224 | tf_op jit(solution)/shard_map/ppermute | solution.py:419
  72.3 9.6 %collective-permute-start.22 = (bf16[512,128]{1,0:T(8,128)(2,1)S(1)}, bf16[512,128]{1,0:T(8,128)(2,1)S(1)}, u32[]{:S(2)}, u32[]{:S(2)}) collective-permute-start(bf16[512,128]{1,0:T(8,128)(2,1)S(1)} %get-tuple-element.60), channel_id=1, source_target_pairs={{0,8},{4,12},{8,0},{12,4},{16,24},{20,28},{24,16},{28,20},{1,9},{5... | collective-permute-start | bytes 393224 | tf_op jit(solution)/shard_map/ppermute | solution.py:419
  72.3 12.2 %collective-permute-start.23 = (bf16[512,128]{1,0:T(8,128)(2,1)S(1)}, bf16[512,128]{1,0:T(8,128)(2,1)S(1)}, u32[]{:S(2)}, u32[]{:S(2)}) collective-permute-start(bf16[512,128]{1,0:T(8,128)(2,1)S(1)} %get-tuple-element.61), channel_id=1, source_target_pairs={{0,12},{4,8},{8,4},{12,0},{16,28},{20,24},{24,20},{28,16},{1,13},{... | collective-permute-start | bytes 393224 | tf_op jit(solution)/shard_map/ppermute | solution.py:419
  74.8 16.8 %collective-permute-start.24 = (bf16[512,128]{1,0:T(8,128)(2,1)S(1)}, bf16[512,128]{1,0:T(8,128)(2,1)S(1)}, u32[]{:S(2)}, u32[]{:S(2)}) collective-permute-start(bf16[512,128]{1,0:T(8,128)(2,1)S(1)} %get-tuple-element.62), channel_id=1, source_target_pairs={{0,16},{4,20},{8,24},{12,28},{16,0},{20,4},{24,8},{28,12},{1,17},{... | collective-permute-start | bytes 393224 | tf_op jit(solution)/shard_map/ppermute | solution.py:419
  77.0 26.5 %collective-permute-start.25 = (bf16[512,128]{1,0:T(8,128)(2,1)S(1)}, bf16[512,128]{1,0:T(8,128)(2,1)S(1)}, u32[]{:S(2)}, u32[]{:S(2)}) collective-permute-start(bf16[512,128]{1,0:T(8,128)(2,1)S(1)} %get-tuple-element.63), channel_id=1, source_target_pairs={{0,20},{4,16},{8,28},{12,24},{16,4},{20,0},{24,12},{28,8},{1,21},{... | collective-permute-start | bytes 393224 | tf_op jit(solution)/shard_map/ppermute | solution.py:419
  78.7 24.7 %collective-permute-start.26 = (bf16[512,128]{1,0:T(8,128)(2,1)S(1)}, bf16[512,128]{1,0:T(8,128)(2,1)S(1)}, u32[]{:S(2)}, u32[]{:S(2)}) collective-permute-start(bf16[512,128]{1,0:T(8,128)(2,1)S(1)} %get-tuple-element.64), channel_id=1, source_target_pairs={{0,24},{4,28},{8,16},{12,20},{16,8},{20,12},{24,0},{28,4},{1,25},{... | collective-permute-start | bytes 393224 | tf_op jit(solution)/shard_map/ppermute | solution.py:419
  81.9 23.3 %collective-permute-start.27 = (bf16[512,128]{1,0:T(8,128)(2,1)S(1)}, bf16[512,128]{1,0:T(8,128)(2,1)S(1)}, u32[]{:S(2)}, u32[]{:S(2)}) collective-permute-start(bf16[512,128]{1,0:T(8,128)(2,1)S(1)} %get-tuple-element.65), channel_id=1, source_target_pairs={{0,28},{4,24},{8,20},{12,16},{16,12},{20,8},{24,4},{28,0},{1,29},{... | collective-permute-start | bytes 393224 | tf_op jit(solution)/shard_map/ppermute | solution.py:419
  84.5 24.0 %collective-permute-start.16 = (bf16[512,128]{1,0:T(8,128)(2,1)S(1)}, bf16[512,128]{1,0:T(8,128)(2,1)S(1)}, u32[]{:S(2)}, u32[]{:S(2)}) collective-permute-start(bf16[512,128]{1,0:T(8,128)(2,1)S(1)} %get-tuple-element.54), channel_id=1, source_target_pairs={{0,12},{4,8},{8,4},{12,0},{16,28},{20,24},{24,20},{28,16},{1,13},{... | collective-permute-start | bytes 393224 | tf_op jit(solution)/shard_map/ppermute | solution.py:419
  91.6 24.2 %collective-permute-start.17 = (bf16[512,128]{1,0:T(8,128)(2,1)S(1)}, bf16[512,128]{1,0:T(8,128)(2,1)S(1)}, u32[]{:S(2)}, u32[]{:S(2)}) collective-permute-start(bf16[512,128]{1,0:T(8,128)(2,1)S(1)} %get-tuple-element.55), channel_id=1, source_target_pairs={{0,16},{4,20},{8,24},{12,28},{16,0},{20,4},{24,8},{28,12},{1,17},{... | collective-permute-start | bytes 393224 | tf_op jit(solution)/shard_map/ppermute | solution.py:419
  103.5 15.2 %collective-permute-start.18 = (bf16[512,128]{1,0:T(8,128)(2,1)S(1)}, bf16[512,128]{1,0:T(8,128)(2,1)S(1)}, u32[]{:S(2)}, u32[]{:S(2)}) collective-permute-start(bf16[512,128]{1,0:T(8,128)(2,1)S(1)} %get-tuple-element.56), channel_id=1, source_target_pairs={{0,20},{4,16},{8,28},{12,24},{16,4},{20,0},{24,12},{28,8},{1,21},{... | collective-permute-start | bytes 393224 | tf_op jit(solution)/shard_map/ppermute | solution.py:419
  103.5 15.2 %collective-permute-start.19 = (bf16[512,128]{1,0:T(8,128)(2,1)S(1)}, bf16[512,128]{1,0:T(8,128)(2,1)S(1)}, u32[]{:S(2)}, u32[]{:S(2)}) collective-permute-start(bf16[512,128]{1,0:T(8,128)(2,1)S(1)} %get-tuple-element.57), channel_id=1, source_target_pairs={{0,24},{4,28},{8,16},{12,20},{16,8},{20,12},{24,0},{28,4},{1,25},{... | collective-permute-start | bytes 393224 | tf_op jit(solution)/shard_map/ppermute | solution.py:419
  105.2 13.5 %collective-permute-start.20 = (bf16[512,128]{1,0:T(8,128)(2,1)S(1)}, bf16[512,128]{1,0:T(8,128)(2,1)S(1)}, u32[]{:S(2)}, u32[]{:S(2)}) collective-permute-start(bf16[512,128]{1,0:T(8,128)(2,1)S(1)} %get-tuple-element.58), channel_id=1, source_target_pairs={{0,28},{4,24},{8,20},{12,16},{16,12},{20,8},{24,4},{28,0},{1,29},{... | collective-permute-start | bytes 393224 | tf_op jit(solution)/shard_map/ppermute | solution.py:419
  119.4 4.7 %collective-permute-start.28 = (f32[1,512]{1,0:T(1,128)S(1)}, f32[1,512]{1,0:T(1,128)S(1)}, u32[]{:S(2)}, u32[]{:S(2)}) collective-permute-start(f32[1,512]{1,0:T(1,128)S(1)} %shard_map.76.refs_0_), channel_id=1, source_target_pairs={{0,3},{1,2},{2,1},{3,0},{4,7},{5,6},{6,5},{7,4},{8,11},{9,10},{10,... | collective-permute-start | bytes 6152 | tf_op jit(solution)/shard_map/ppermute | solution.py:473
  119.5 4.6 %collective-permute-start.29 = (f32[1,512]{1,0:T(1,128)S(1)}, f32[1,512]{1,0:T(1,128)S(1)}, u32[]{:S(2)}, u32[]{:S(2)}) collective-permute-start(f32[1,512]{1,0:T(1,128)S(1)} %shard_map.76.refs_0_), channel_id=1, source_target_pairs={{0,2},{1,3},{2,0},{3,1},{4,6},{5,7},{6,4},{7,5},{8,10},{9,11},{10,... | collective-permute-start | bytes 6152 | tf_op jit(solution)/shard_map/ppermute | solution.py:473
  121.1 3.0 %collective-permute-start.30 = (f32[1,512]{1,0:T(1,128)S(1)}, f32[1,512]{1,0:T(1,128)S(1)}, u32[]{:S(2)}, u32[]{:S(2)}) collective-permute-start(f32[1,512]{1,0:T(1,128)S(1)} %shard_map.76.refs_0_), channel_id=1, source_target_pairs={{0,1},{1,0},{2,3},{3,2},{4,5},{5,4},{6,7},{7,6},{8,9},{9,8},{10,11... | collective-permute-start | bytes 6152 | tf_op jit(solution)/shard_map/ppermute | solution.py:473
  122.7 1.4 %copy-start.1 = (f32[2048]{0:T(1024)S(1)}, f32[2048]{0:T(1024)}, u32[]{:S(2)}) copy-start(f32[2048]{0:T(1024)} %param.9) | copy-start | bytes 24580
